TPU v7x, 32 devices: a whole 2x2x4 slice. The times are simulated.
32 devices in a mesh: swath: 8 (over y, x, core), chan: 4 (over z).
Axes of the slice: x: 2, y: 2, z: 4, core: 2. Of those that a mesh axis runs over, the one named last changes fastest.
Arguments:
- innovations: float32 [524288], P(('swath', 'chan')), may hold values from -6 to 6
- obs_precision: float32 [524288], P(('swath', 'chan')), may hold values from 0.25 to 4
- jacobian: bfloat16 [524288, 128], P(('swath', 'chan')), may hold values from -0.5 to 0.5
- predictors: float32 [8, 524288], P(None, ('swath', 'chan')), may hold values from -5 to 5
- obs_column: int32 [524288], P(('swath', 'chan')), may hold values from 0 to 2047, as said below
- obs_channel: int32 [524288], P(('swath', 'chan')), may hold values from 0 to 5119
- obs_count: int32 [8, 4], P('swath', 'chan'), may hold values from 5461 to 16384, as said below
- smoothing: float32 [128], replicated, may hold values from 0.02 to 0.12
- bias_precision: float32 [8, 5120], P(None, 'chan'), may hold values from 1 to 100
Outputs:
- control_state: float32 [256, 256, 128], P('swath', 'chan')
- bias_increment: float32 [8, 5120], P(None, 'chan')
- residual_norms: float32 [3], replicated
Inputs may be any that keep to these rules, and one draw needn't show every extreme that they name: `obs_column`: Row-major index latitude row * 64 + longitude column within the tile of the device that holds the slot; all slots of an aligned block of 128 slots lie in one latitude row. `obs_channel`: channel c belongs to block c // 256, whose coefficients are owned by chan index c // 1280. `obs_count`: slots below the count hold live observations, the rest are ignored; some device is full in every draw.
All inputs are finite; a program needn't handle non-finite values.
Results may differ from a plain program's by a relative error of at most 0.0003.
Values sent between devices are 32-bit elements; how exact they have to be, the bound alone decides.
A program may use at most 128 MiB of HBM per device.

v0:
```python
import jax
import jax.numpy as jnp
from jax import lax
from jax.sharding import PartitionSpec as P

LEV = 128
NPRED = 8
CH_BLOCK = 256
OBS_BLOCK = 128
LAT_DEV = 32
LON_DEV = 64
ITERS = 2


def with_halo(array, sides, width):
    for axis, dim in sides:
        size, length = (lax.axis_size(axis), array.shape[dim])
        up = [(i, (i + 1) % size) for i in range(size)]
        down = [(j, i) for i, j in up]
        last = lax.slice_in_dim(array, length - width, length, axis=dim)
        leading = lax.slice_in_dim(array, 0, width, axis=dim)
        before = lax.ppermute(last, axis, up)
        after = lax.ppermute(leading, axis, down)
        array = jnp.concatenate([before, array, after], axis=dim)
    return array


def body(
    innovations,
    obs_precision,
    jacobian,
    predictors,
    obs_column,
    obs_channel,
    obs_count,
    smoothing,
    bias_precision,
):
    owned_width = bias_precision.shape[1]
    channels_all = owned_width * lax.axis_size("chan")
    block_ids = channels_all // CH_BLOCK
    slot_total = obs_precision.shape[0]
    line_count = slot_total // OBS_BLOCK
    band_index = lax.axis_index("swath")
    top_keep = band_index > 0
    bottom_keep = band_index < lax.axis_size("swath") - 1
    bias_weight = jnp.where(band_index == 0, 1.0, 0.0).astype(jnp.float32)
    live = jnp.arange(slot_total, dtype=jnp.int32) < obs_count[0, 0]
    weights = jnp.where(live, obs_precision, 0.0)
    row_ids = jnp.arange(LAT_DEV)
    keep_above = ((row_ids > 0) | top_keep)[:, None, None]
    keep_below = ((row_ids < LAT_DEV - 1) | bottom_keep)[:, None, None]
    highest = lax.Precision.HIGHEST
    line_cells = obs_column.reshape(line_count, OBS_BLOCK)
    line_row = line_cells[:, 0] // LON_DEV
    row_hot = (line_row[:, None] == jnp.arange(LAT_DEV, dtype=jnp.int32)[None, :]).astype(
        jnp.float32
    )
    col_hot = (
        (line_cells % LON_DEV)[:, :, None] == jnp.arange(LON_DEV, dtype=jnp.int32)[None, None, :]
    ).astype(jnp.float32)
    jac_lines = jacobian.reshape(line_count, OBS_BLOCK, LEV).astype(jnp.float32)
    block_hot = (
        (obs_channel // CH_BLOCK)[:, None] == jnp.arange(block_ids, dtype=jnp.int32)[None, :]
    ).astype(jnp.float32)
    inner_hot = (
        (obs_channel % CH_BLOCK)[:, None] == jnp.arange(CH_BLOCK, dtype=jnp.int32)[None, :]
    ).astype(jnp.float32)

    def smooth_local(state_field):
        padded = with_halo(state_field, (("swath", 0), ("chan", 1)), 1)
        above_row = jnp.where(keep_above, padded[:-2, 1:-1], 0.0)
        below_row = jnp.where(keep_below, padded[2:, 1:-1], 0.0)
        beside = above_row + below_row + padded[1:-1, :-2] + padded[1:-1, 2:]
        return state_field + smoothing * (beside - 4.0 * state_field)

    def adjoint(values):
        terms = jac_lines * values.reshape(line_count, OBS_BLOCK)[:, :, None]
        line_fields = jnp.einsum("box,bok->bxk", col_hot, terms, precision=highest)
        return jnp.einsum("bl,bxk->lxk", row_hot, line_fields, precision=highest)

    def partial_table(terms):
        rows_in = terms.shape[0]
        spread = (terms[:, None, :] * block_hot.T[None, :, :]).reshape(
            rows_in * block_ids, slot_total
        )
        table = jnp.dot(spread, inner_hot, precision=highest)
        return table.reshape(rows_in, channels_all)

    def to_owners(partial_value):
        owned = lax.psum_scatter(partial_value, "chan", scatter_dimension=1, tiled=True)
        return lax.psum(owned, "swath")

    def inner(state_one, state_two, bias_one, bias_two):
        return jnp.sum(state_one * state_two) + bias_weight * jnp.sum(bias_one * bias_two)

    source = weights * innovations
    stacked = to_owners(
        partial_table(
            jnp.concatenate(
                [predictors * source[None, :], predictors * predictors * weights[None, :]], axis=0
            )
        )
    )
    res_state = smooth_local(adjoint(source))
    res_bias = stacked[:NPRED]
    diagonal = bias_precision + stacked[NPRED:]
    sol_state = jnp.zeros_like(res_state)
    sol_bias = jnp.zeros_like(res_bias)
    pre_bias = res_bias / diagonal
    record = []

    def norms_of(state_res, bias_res, bias_pre):
        return lax.psum(
            (
                inner(state_res, state_res, bias_res, bias_pre),
                inner(state_res, state_res, bias_res, bias_res),
            ),
            ("swath", "chan"),
        )

    rz_now, rr_now = norms_of(res_state, res_bias, pre_bias)
    record.append(rr_now)
    dir_state, dir_bias = (res_state, pre_bias)
    for turn_index in range(ITERS):
        smoothed = smooth_local(dir_state)
        hessian_everything = lax.all_gather(dir_bias, "chan", axis=1, tiled=True)
        flat = hessian_everything.reshape(NPRED * block_ids, CH_BLOCK)
        mid = jnp.dot(inner_hot, flat.T, precision=highest).reshape(slot_total, NPRED, block_ids)
        looked = jnp.sum(mid * predictors.T[:, :, None] * block_hot[:, None, :], axis=(1, 2))
        forward_line_fields = jnp.einsum("bl,lxk->bxk", row_hot, smoothed, precision=highest)
        picked = jnp.einsum("box,bxk->bok", col_hot, forward_line_fields, precision=highest)
        image = weights * (jnp.sum(jac_lines * picked, axis=2).reshape(-1) + looked)
        state_out = dir_state + smooth_local(adjoint(image))
        bias_out = bias_precision * dir_bias + to_owners(partial_table(predictors * image[None, :]))
        curve = lax.psum(inner(dir_state, state_out, dir_bias, bias_out), ("swath", "chan"))
        length = rz_now / curve
        sol_state = sol_state + length * dir_state
        sol_bias = sol_bias + length * dir_bias
        res_state = res_state - length * state_out
        res_bias = res_bias - length * bias_out
        pre_bias = res_bias / diagonal
        rz_next, rr_now = norms_of(res_state, res_bias, pre_bias)
        record.append(rr_now)
        ratio = rz_next / rz_now
        dir_state = res_state + ratio * dir_state
        dir_bias = pre_bias + ratio * dir_bias
        rz_now = rz_next
    return (sol_state, sol_bias, jnp.sqrt(jnp.stack(record)))


def solution(mesh):
    placed = (
        P(("swath", "chan")),
        P(("swath", "chan")),
        P(("swath", "chan"), None),
        P(None, ("swath", "chan")),
        P(("swath", "chan")),
        P(("swath", "chan")),
        P("swath", "chan"),
        P(),
        P(None, "chan"),
    )
    return jax.shard_map(
        body,
        mesh=mesh,
        in_specs=placed,
        out_specs=(P("swath", "chan", None), P(None, "chan"), P()),
        check_vma=False,
    )
```

profile of v0, /device:TPU:0, one launch (start us, length us, event | category | flops | bytes accessed | tf_op | source)
XLA Modules:
  0.0 604.4 jit_solution(15087410023057047075)
XLA Ops:
  10.6 7.1 %fusion.17 = f32[128,64,128]{2,1,0:T(8,128)S(1)} fusion(bf16[128,128,128]{2,1,0:T(8,128)(2,1)} %bitcast.41, f32[128,128]{1,0:T(8,128)S(1)} %bitcast.49, s32[128,128]{1,0:T(8,128)S(1)} %add_select_fusion.2), kind=kOutput, calls=%fused_computation.21 | convolution fusion | flops 1615855616 | bytes 8519680 | tf_op jit(solution)/shard_map/box,bok->bxk/dot_general | solution.py:79
  26.0 8.5 %broadcast_multiply_fusion = f32[16,20,16384]{2,1,0:T(8,128)} fusion(f32[20,16384]{1,0:T(8,128)S(1)} %fusion.50, f32[16,16384]{1,0:T(8,128)S(1)} %pad_maximum_fusion.48), kind=kLoop, calls=%fused_computation.9 | loop fusion | flops 5242880 | bytes 23330816 | tf_op jit(solution)/shard_map/mul | solution.py:84
  38.8 17.1 %mul.337 = f32[320,16384]{1,0:T(8,128)} reshape(f32[16,20,16384]{2,1,0:T(8,128)} %broadcast_multiply_fusion) | data formatting | bytes 41943040 | tf_op jit(solution)/shard_map/mul | solution.py:84
  60.5 16.8 %fusion.5 = f32[320,256]{1,0:T(8,128)} fusion(f32[320,16384]{1,0:T(8,128)} %mul.337, s32[16384]{0:T(1024)S(1)} %get-tuple-element.55), kind=kOutput, calls=%fused_computation.8 | convolution fusion | flops 16110321664 | bytes 21364736 | tf_op jit(solution)/shard_map/dot_general | solution.py:87
  85.3 7.0 %copy.21 = f32[128,128,128]{1,2,0:T(8,128)} copy(bf16[128,128,128]{2,1,0:T(8,128)(2,1)} %bitcast.42) | data formatting | bytes 12582912 | tf_op jit(solution)/shard_map/convert_element_type | solution.py:62
  92.3 7.2 %fusion.91 = f32[128,64,128]{2,0,1:T(8,128)} fusion(f32[32,64,128]{2,0,1:T(8,128)} %copy-done.9, f32[34,1,128]{2,0,1:T(8,128)} %collective-permute-done.7, f32[1,64,128]{2,0,1:T(1,128)S(1)} %collective-permute-done.5, f32[1,64,128]{2,0,1:T(1,128)} %collective-permute-done.4, f32[34,1,128]{2,0,1:T(8,128)} %collective-permute-done.6, f32[128]{0:T(128)S(1)} %copy-done.31, ...), kind=kOutput, calls=%fused_computation.113 | convolution fusion | flops 407113728 | bytes 5344320 | tf_op jit(solution)/shard_map/bl,lxk->bxk/dot_general | solution.py:131
  101.3 11.4 %multiply_reduce_fusion.1 = f32[128,128]{1,0:T(8,128)S(1)} fusion(f32[128,128,128]{1,2,0:T(8,128)} %copy.21, f32[128,64,128]{2,0,1:T(8,128)} %fusion.91, s32[128,128]{1,0:T(8,128)S(1)} %add_select_fusion.2), kind=kOutput, calls=%fused_computation.15 | convolution fusion | flops 1615839232 | bytes 12713984 | tf_op jit(solution)/shard_map/box,bxk->bok/dot_general | solution.py:132
  112.7 40.4 %all-reduce.4.cloned.1.call-done = f32[16,1280]{1,0:T(8,128)} async-done(((f32[16,1280]{1,0:T(8,128)}), f32[16,1280]{1,0:T(8,128)}) %all-reduce.4.cloned.1.call-update) | async-done | bytes 81936 | tf_op jit(solution)/shard_map/psum | solution.py:92
  153.9 14.0 %all_gather.6 = f32[8,5120]{1,0:T(8,128)S(1)} all-gather(f32[8,1280]{1,0:T(8,128)S(1)} %slice_divide_fusion), channel_id=1, replica_groups=mesh['swath'=8,'chan'=4] {'chan'}, dimensions={1}, use_global_device_ids=true | all-gather | bytes 204800 | tf_op jit(solution)/shard_map/all_gather | solution.py:127
  167.9 12.2 %fusion.35 = f32[16384]{0:T(1024)S(1)} fusion(f32[16384,20]{0,1:T(8,128)} %fusion.51, f32[16384,8]{0,1:T(8,128)S(1)} %bitcast.45, s32[16384]{0:T(1024)S(1)} %get-tuple-element.55, f32[8,20,256]{2,0,1:T(8,128)S(1)} %bitcast.52), kind=kOutput, calls=%fused_computation.42 | convolution fusion | flops 8065105920 | bytes 2129920 | tf_op jit(solution)/shard_map/dot_general | solution.py:129
  180.3 5.9 fusion.10
  192.2 5.9 broadcast_multiply_fusion.2
  198.1 8.7 %mul.360 = f32[160,16384]{1,0:T(8,128)} reshape(f32[8,20,16384]{2,1,0:T(8,128)} %broadcast_multiply_fusion.2) | data formatting | bytes 20971520 | tf_op jit(solution)/shard_map/mul | solution.py:84
  212.0 11.9 %fusion.3 = f32[160,256]{1,0:T(8,128)} fusion(f32[160,16384]{1,0:T(8,128)} %mul.360, s32[16384]{0:T(1024)S(1)} %get-tuple-element.55), kind=kOutput, calls=%fused_computation.6 | convolution fusion | flops 8057257984 | bytes 10715136 | tf_op jit(solution)/shard_map/dot_general | solution.py:87
  225.8 6.8 %multiply_reduce_fusion.5 = (f32[]{:T(128)}, f32[]{:T(128)}, f32[32,64,128]{2,0,1:T(8,128)}) fusion(f32[32,64,128]{2,0,1:T(8,128)} %copy-done.5, f32[34,1,128]{2,0,1:T(8,128)} %collective-permute-done.11, f32[1,64,128]{2,0,1:T(1,128)} %copy-done.18, f32[1,64,128]{2,0,1:T(1,128)} %copy-done.19, f32[34,1,128]{2,0,1:T(8,128)} %collective-permute-done.10, ...), kind=kLoop, calls=%fused_computation.153 | loop fusion | flops 10223614 | bytes 3347016 | tf_op jit(solution)/shard_map/reduce_sum | solution.py:95
  232.6 13.9 %reduce-scatter.6.cloned.1.call-done = f32[8,1280]{1,0:T(8,128)} async-done(((f32[8,5120]{1,0:T(8,128)}), f32[8,1280]{1,0:T(8,128)}) %reduce-scatter.6.cloned.1.call-update) | async-done | bytes 40976 | tf_op jit(solution)/shard_map/reduce_scatter | solution.py:91
  246.5 23.9 %psum.72 = f32[8,1280]{1,0:T(8,128)} all-reduce(f32[8,1280]{1,0:T(8,128)} %reduce-scatter.6.cloned.1.call-done), channel_id=1, replica_groups=mesh['swath'=8,'chan'=4] {'swath'}, use_global_device_ids=true, to_apply=%region_9.10 | all-reduce | flops 10240 | bytes 81920 | tf_op jit(solution)/shard_map/psum | solution.py:92
  274.5 37.6 %all-reduce.1 = (f32[]{:T(128)}, f32[]{:T(128)}) all-reduce(f32[]{:T(128)S(6)} %add.166, f32[]{:T(128)S(6)} %add.178), channel_id=1, replica_groups=mesh['swath'=8,'chan'=4] {'swath','chan'}, use_global_device_ids=true, to_apply=%region_4.5 | all-reduce | flops 2 | bytes 16 | tf_op jit(solution)/shard_map/psum | solution.py:114
  319.4 42.3 %psum.74 = f32[]{:T(128)} all-reduce(f32[]{:T(128)S(6)} %add.179), channel_id=1, replica_groups=mesh['swath'=8,'chan'=4] {'swath','chan'}, use_global_device_ids=true, to_apply=%region_14.15 | all-reduce | flops 1 | bytes 8 | tf_op jit(solution)/shard_map/psum | solution.py:114
  367.1 13.7 %all_gather.7 = f32[8,5120]{1,0:T(8,128)S(1)} all-gather(f32[8,1280]{1,0:T(8,128)S(1)} %multiply_add_fusion.4), channel_id=1, replica_groups=mesh['swath'=8,'chan'=4] {'chan'}, dimensions={1}, use_global_device_ids=true | all-gather | bytes 204800 | tf_op jit(solution)/shard_map/all_gather | solution.py:127
  384.1 11.7 %fusion.38 = f32[16384]{0:T(1024)} fusion(f32[16384,20]{0,1:T(8,128)S(1)} %copy-done.10, f32[16384,8]{0,1:T(8,128)S(1)} %bitcast.46, s32[16384]{0:T(1024)S(1)} %get-tuple-element.55, f32[8,20,256]{2,0,1:T(8,128)S(1)} %bitcast.51), kind=kOutput, calls=%fused_computation.43 | convolution fusion | flops 8065105920 | bytes 2129920 | tf_op jit(solution)/shard_map/dot_general | solution.py:129
  396.5 5.3 fusion.65
  401.8 11.9 %multiply_reduce_fusion = f32[128,128]{1,0:T(8,128)S(1)} fusion(f32[128,128,128]{1,2,0:T(8,128)} %copy.21, f32[128,64,128]{2,0,1:T(8,128)S(1)} %fusion.65, s32[128,128]{1,0:T(8,128)S(1)} %add_select_fusion.2), kind=kOutput, calls=%fused_computation.12 | convolution fusion | flops 1615839232 | bytes 12713984 | tf_op jit(solution)/shard_map/box,bxk->bok/dot_general | solution.py:132
  413.8 5.9 fusion.8
  425.2 5.9 broadcast_multiply_fusion.1
  431.1 8.8 %mul.392 = f32[160,16384]{1,0:T(8,128)} reshape(f32[8,20,16384]{2,1,0:T(8,128)} %broadcast_multiply_fusion.1) | data formatting | bytes 20971520 | tf_op jit(solution)/shard_map/mul | solution.py:84
  444.3 12.0 %fusion.2 = f32[160,256]{1,0:T(8,128)} fusion(f32[160,16384]{1,0:T(8,128)} %mul.392, s32[16384]{0:T(1024)S(1)} %get-tuple-element.55), kind=kOutput, calls=%fused_computation.5 | convolution fusion | flops 8057257984 | bytes 10715136 | tf_op jit(solution)/shard_map/dot_general | solution.py:87
  458.1 5.6 multiply_reduce_fusion.3
  463.7 15.0 %reduce-scatter.8.cloned.1.call-done = f32[8,1280]{1,0:T(8,128)} async-done(((f32[8,5120]{1,0:T(8,128)}), f32[8,1280]{1,0:T(8,128)}) %reduce-scatter.8.cloned.1.call-update) | async-done | bytes 40976 | tf_op jit(solution)/shard_map/reduce_scatter | solution.py:91
  478.7 23.3 %psum.75 = f32[8,1280]{1,0:T(8,128)S(1)} all-reduce(f32[8,1280]{1,0:T(8,128)} %reduce-scatter.8.cloned.1.call-done), channel_id=1, replica_groups=mesh['swath'=8,'chan'=4] {'swath'}, use_global_device_ids=true, to_apply=%region_19.20 | all-reduce | flops 10240 | bytes 81920 | tf_op jit(solution)/shard_map/psum | solution.py:92
  504.4 37.5 %psum.76 = f32[]{:T(128)} all-reduce(f32[]{:T(128)S(6)} %add.193), channel_id=1, replica_groups=mesh['swath'=8,'chan'=4] {'swath','chan'}, use_global_device_ids=true, to_apply=%region_21.22 | all-reduce | flops 1 | bytes 8 | tf_op jit(solution)/shard_map/psum | solution.py:136
  551.5 43.7 %all-reduce = (f32[1]{0:T(128)}, f32[1]{0:T(128)}, f32[1]{0:T(128)}) all-reduce(f32[1]{0:T(128)} %bitcast.16, f32[1]{0:T(128)} %bitcast.15, f32[1]{0:T(128)} %bitcast.14), channel_id=1, replica_groups=mesh['swath'=8,'chan'=4] {'swath','chan'}, use_global_device_ids=true, to_apply=%region_28.29 | all-reduce | flops 3 | bytes 24 | tf_op jit(solution)/shard_map/psum | solution.py:114
  (166 shorter events, 77.1 us)
Async XLA Ops:
  7.2 94.0 %reduce-scatter.4.cloned.1.call-start = ((), (), s32[]{:S(2)}) async-start(), calls=%async_computation.3 | async-start | bytes 409600 | tf_op jit(solution)/shard_map/reduce_scatter | solution.py:91
  22.3 12.2 %collective-permute-start.1 = (f32[1,64,128]{2,0,1:T(1,128)}, f32[1,64,128]{2,0,1:T(1,128)S(1)}, u32[]{:S(2)}, u32[]{:S(2)}) collective-permute-start(f32[1,64,128]{2,0,1:T(1,128)} %get-tuple-element.52), channel_id=1, source_target_pairs={{4,0},{8,4},{12,8},{16,12},{20,16},{24,20},{28,24},{0,28},{5,1},{9... | collective-permute-start | bytes 98312 | tf_op jit(solution)/shard_map/ppermute | solution.py:23
  25.7 8.9 %collective-permute-start = (f32[1,64,128]{2,0,1:T(1,128)}, f32[1,64,128]{2,0,1:T(1,128)S(1)}, u32[]{:S(2)}, u32[]{:S(2)}) collective-permute-start(f32[1,64,128]{2,0,1:T(1,128)} %get-tuple-element.51), channel_id=1, source_target_pairs={{0,4},{4,8},{8,12},{12,16},{16,20},{20,24},{24,28},{28,0},{1,5},{5... | collective-permute-start | bytes 98312 | tf_op jit(solution)/shard_map/ppermute | solution.py:22
  35.2 20.7 %collective-permute-start.3 = (f32[34,1,128]{2,0,1:T(8,128)}, f32[34,1,128]{2,0,1:T(8,128)S(1)}, u32[]{:S(2)}, u32[]{:S(2)}) collective-permute-start(f32[34,1,128]{2,0,1:T(8,128)} %get-tuple-element.40), channel_id=1, source_target_pairs={{1,0},{2,1},{3,2},{0,3},{5,4},{6,5},{7,6},{4,7},{9,8},{10,9},{11,1... | collective-permute-start | bytes 52232 | tf_op jit(solution)/shard_map/ppermute | solution.py:23
  38.8 17.1 %collective-permute-start.2 = (f32[34,1,128]{2,0,1:T(8,128)S(1)}, f32[34,1,128]{2,0,1:T(8,128)S(1)}, u32[]{:S(2)}, u32[]{:S(2)}) collective-permute-start(f32[34,1,128]{2,0,1:T(8,128)S(1)} %get-tuple-element.39), channel_id=1, source_target_pairs={{0,1},{1,2},{2,3},{3,0},{4,5},{5,6},{6,7},{7,4},{8,9},{9,10},{10,1... | collective-permute-start | bytes 52232 | tf_op jit(solution)/shard_map/ppermute | solution.py:22
  38.8 53.5 %copy-start.25 = (pred[32]{0:T(512)(128)(4,1)}, pred[32]{0:T(512)(128)(4,1)S(1)}, u32[]{:S(2)}) copy-start(pred[32]{0:T(512)(128)(4,1)S(1)} %get-tuple-element.58) | copy-start | bytes 100
  38.8 53.5 %copy-start.27 = (pred[32]{0:T(512)(128)(4,1)}, pred[32]{0:T(512)(128)(4,1)S(1)}, u32[]{:S(2)}) copy-start(pred[32]{0:T(512)(128)(4,1)S(1)} %get-tuple-element.59) | copy-start | bytes 100
  55.9 21.4 %copy-start.12 = (f32[34,1,128]{2,0,1:T(8,128)}, f32[34,1,128]{2,0,1:T(8,128)S(1)}, u32[]{:S(2)}) copy-start(f32[34,1,128]{2,0,1:T(8,128)S(1)} %collective-permute-done.3) | copy-start | bytes 52228
  58.1 21.1 %collective-permute-start.5 = (f32[1,64,128]{2,0,1:T(1,128)}, f32[1,64,128]{2,0,1:T(1,128)S(1)}, u32[]{:S(2)}, u32[]{:S(2)}) collective-permute-start(f32[1,64,128]{2,0,1:T(1,128)} %get-tuple-element.50), channel_id=1, source_target_pairs={{4,0},{8,4},{12,8},{16,12},{20,16},{24,20},{28,24},{0,28},{5,1},{9... | collective-permute-start | bytes 98312 | tf_op jit(solution)/shard_map/ppermute | solution.py:23
  60.5 18.7 %collective-permute-start.4 = (f32[1,64,128]{2,0,1:T(1,128)}, f32[1,64,128]{2,0,1:T(1,128)}, u32[]{:S(2)}, u32[]{:S(2)}) collective-permute-start(f32[1,64,128]{2,0,1:T(1,128)} %get-tuple-element.49), channel_id=1, source_target_pairs={{0,4},{4,8},{8,12},{12,16},{16,20},{20,24},{24,28},{28,0},{1,5},{5... | collective-permute-start | bytes 98312 | tf_op jit(solution)/shard_map/ppermute | solution.py:22
  79.1 74.0 %all-reduce.4.cloned.1.call-start = ((), (), s32[]{:S(2)}) async-start(), calls=%async_computation.4 | async-start | bytes 163840 | tf_op jit(solution)/shard_map/psum | solution.py:92
  79.9 12.3 %collective-permute-start.7 = (f32[34,1,128]{2,0,1:T(8,128)S(1)}, f32[34,1,128]{2,0,1:T(8,128)}, u32[]{:S(2)}, u32[]{:S(2)}) collective-permute-start(f32[34,1,128]{2,0,1:T(8,128)S(1)} %get-tuple-element.38), channel_id=1, source_target_pairs={{1,0},{2,1},{3,2},{0,3},{5,4},{6,5},{7,6},{4,7},{9,8},{10,9},{11,1... | collective-permute-start | bytes 52232 | tf_op jit(solution)/shard_map/ppermute | solution.py:23
  83.5 8.7 %collective-permute-start.6 = (f32[34,1,128]{2,0,1:T(8,128)S(1)}, f32[34,1,128]{2,0,1:T(8,128)}, u32[]{:S(2)}, u32[]{:S(2)}) collective-permute-start(f32[34,1,128]{2,0,1:T(8,128)S(1)} %get-tuple-element.37), channel_id=1, source_target_pairs={{0,1},{1,2},{2,3},{3,0},{4,5},{5,6},{6,7},{7,4},{8,9},{9,10},{10,1... | collective-permute-start | bytes 52232 | tf_op jit(solution)/shard_map/ppermute | solution.py:22
  101.2 51.9 %copy-start.11 = (f32[8,1280]{1,0:T(8,128)S(1)}, f32[8,1280]{1,0:T(8,128)}, u32[]{:S(2)}) copy-start(f32[8,1280]{1,0:T(8,128)} %param.17) | copy-start | bytes 122884
  101.2 145.2 %reduce-scatter.6.cloned.1.call-start = ((), (), s32[]{:S(2)}) async-start(), calls=%async_computation.5 | async-start | bytes 204800 | tf_op jit(solution)/shard_map/reduce_scatter | solution.py:91
  191.7 15.1 %collective-permute-start.9 = (f32[1,64,128]{2,0,1:T(1,128)}, f32[1,64,128]{2,0,1:T(1,128)S(1)}, u32[]{:S(2)}, u32[]{:S(2)}) collective-permute-start(f32[1,64,128]{2,0,1:T(1,128)} %get-tuple-element.48), channel_id=1, source_target_pairs={{4,0},{8,4},{12,8},{16,12},{20,16},{24,20},{28,24},{0,28},{5,1},{9... | collective-permute-start | bytes 98312 | tf_op jit(solution)/shard_map/ppermute | solution.py:23
  191.7 15.1 %collective-permute-start.8 = (f32[1,64,128]{2,0,1:T(1,128)}, f32[1,64,128]{2,0,1:T(1,128)S(1)}, u32[]{:S(2)}, u32[]{:S(2)}) collective-permute-start(f32[1,64,128]{2,0,1:T(1,128)} %get-tuple-element.47), channel_id=1, source_target_pairs={{0,4},{4,8},{8,12},{12,16},{16,20},{20,24},{24,28},{28,0},{1,5},{5... | collective-permute-start | bytes 98312 | tf_op jit(solution)/shard_map/ppermute | solution.py:22
  208.3 17.4 %collective-permute-start.11 = (f32[34,1,128]{2,0,1:T(8,128)}, f32[34,1,128]{2,0,1:T(8,128)}, u32[]{:S(2)}, u32[]{:S(2)}) collective-permute-start(f32[34,1,128]{2,0,1:T(8,128)} %get-tuple-element.36), channel_id=1, source_target_pairs={{1,0},{2,1},{3,2},{0,3},{5,4},{6,5},{7,6},{4,7},{9,8},{10,9},{11,1... | collective-permute-start | bytes 52232 | tf_op jit(solution)/shard_map/ppermute | solution.py:23
  211.8 13.9 %collective-permute-start.10 = (f32[34,1,128]{2,0,1:T(8,128)}, f32[34,1,128]{2,0,1:T(8,128)}, u32[]{:S(2)}, u32[]{:S(2)}) collective-permute-start(f32[34,1,128]{2,0,1:T(8,128)} %get-tuple-element.35), channel_id=1, source_target_pairs={{0,1},{1,2},{2,3},{3,0},{4,5},{5,6},{6,7},{7,4},{8,9},{9,10},{10,1... | collective-permute-start | bytes 52232 | tf_op jit(solution)/shard_map/ppermute | solution.py:22
  225.6 253.1 %reduce-scatter.8.cloned.1.call-start = ((), (), s32[]{:S(2)}) async-start(), calls=%async_computation.6 | async-start | bytes 204800 | tf_op jit(solution)/shard_map/reduce_scatter | solution.py:91
  365.0 30.8 %copy-start.2 = (f32[32,64,128]{2,0,1:T(8,128)}, f32[32,64,128]{2,0,1:T(8,128)S(1)}, u32[]{:S(2)}) copy-start(f32[32,64,128]{2,0,1:T(8,128)S(1)} %multiply_add_fusion.1) | copy-start | bytes 3145732
  365.1 15.7 %collective-permute-start.13 = (f32[1,64,128]{2,0,1:T(1,128)S(1)}, f32[1,64,128]{2,0,1:T(1,128)S(1)}, u32[]{:S(2)}, u32[]{:S(2)}) collective-permute-start(f32[1,64,128]{2,0,1:T(1,128)S(1)} %get-tuple-element.46), channel_id=1, source_target_pairs={{4,0},{8,4},{12,8},{16,12},{20,16},{24,20},{28,24},{0,28},{5,1},{9... | collective-permute-start | bytes 98312 | tf_op jit(solution)/shard_map/ppermute | solution.py:23
  366.3 14.5 %collective-permute-start.12 = (f32[1,64,128]{2,0,1:T(1,128)S(1)}, f32[1,64,128]{2,0,1:T(1,128)S(1)}, u32[]{:S(2)}, u32[]{:S(2)}) collective-permute-start(f32[1,64,128]{2,0,1:T(1,128)S(1)} %get-tuple-element.45), channel_id=1, source_target_pairs={{0,4},{4,8},{8,12},{12,16},{16,20},{20,24},{24,28},{28,0},{1,5},{5... | collective-permute-start | bytes 98312 | tf_op jit(solution)/shard_map/ppermute | solution.py:22
  382.1 14.4 %collective-permute-start.15 = (f32[34,1,128]{2,0,1:T(8,128)}, f32[34,1,128]{2,0,1:T(8,128)}, u32[]{:S(2)}, u32[]{:S(2)}) collective-permute-start(f32[34,1,128]{2,0,1:T(8,128)} %get-tuple-element.34), channel_id=1, source_target_pairs={{1,0},{2,1},{3,2},{0,3},{5,4},{6,5},{7,6},{4,7},{9,8},{10,9},{11,1... | collective-permute-start | bytes 52232 | tf_op jit(solution)/shard_map/ppermute | solution.py:23
  383.7 12.8 %collective-permute-start.14 = (f32[34,1,128]{2,0,1:T(8,128)}, f32[34,1,128]{2,0,1:T(8,128)}, u32[]{:S(2)}, u32[]{:S(2)}) collective-permute-start(f32[34,1,128]{2,0,1:T(8,128)} %get-tuple-element.33), channel_id=1, source_target_pairs={{0,1},{1,2},{2,3},{3,0},{4,5},{5,6},{6,7},{7,4},{8,9},{9,10},{10,1... | collective-permute-start | bytes 52232 | tf_op jit(solution)/shard_map/ppermute | solution.py:22
  424.7 15.3 %collective-permute-start.17 = (f32[1,64,128]{2,0,1:T(1,128)S(1)}, f32[1,64,128]{2,0,1:T(1,128)S(1)}, u32[]{:S(2)}, u32[]{:S(2)}) collective-permute-start(f32[1,64,128]{2,0,1:T(1,128)S(1)} %get-tuple-element.44), channel_id=1, source_target_pairs={{4,0},{8,4},{12,8},{16,12},{20,16},{24,20},{28,24},{0,28},{5,1},{9... | collective-permute-start | bytes 98312 | tf_op jit(solution)/shard_map/ppermute | solution.py:23
  424.7 15.2 %collective-permute-start.16 = (f32[1,64,128]{2,0,1:T(1,128)S(1)}, f32[1,64,128]{2,0,1:T(1,128)S(1)}, u32[]{:S(2)}, u32[]{:S(2)}) collective-permute-start(f32[1,64,128]{2,0,1:T(1,128)S(1)} %get-tuple-element.43), channel_id=1, source_target_pairs={{0,4},{4,8},{8,12},{12,16},{16,20},{20,24},{24,28},{28,0},{1,5},{5... | collective-permute-start | bytes 98312 | tf_op jit(solution)/shard_map/ppermute | solution.py:22
  440.6 17.4 %collective-permute-start.19 = (f32[34,1,128]{2,0,1:T(8,128)}, f32[34,1,128]{2,0,1:T(8,128)S(1)}, u32[]{:S(2)}, u32[]{:S(2)}) collective-permute-start(f32[34,1,128]{2,0,1:T(8,128)} %get-tuple-element.32), channel_id=1, source_target_pairs={{1,0},{2,1},{3,2},{0,3},{5,4},{6,5},{7,6},{4,7},{9,8},{10,9},{11,1... | collective-permute-start | bytes 52232 | tf_op jit(solution)/shard_map/ppermute | solution.py:23
  444.0 99.3 %copy-start.17 = (f32[8,1280]{1,0:T(8,128)S(1)}, f32[8,1280]{1,0:T(8,128)}, u32[]{:S(2)}) copy-start(f32[8,1280]{1,0:T(8,128)} %get-tuple-element.27) | copy-start | bytes 122884
  444.0 14.0 %collective-permute-start.18 = (f32[34,1,128]{2,0,1:T(8,128)}, f32[34,1,128]{2,0,1:T(8,128)}, u32[]{:S(2)}, u32[]{:S(2)}) collective-permute-start(f32[34,1,128]{2,0,1:T(8,128)} %get-tuple-element.31), channel_id=1, source_target_pairs={{0,1},{1,2},{2,3},{3,0},{4,5},{5,6},{6,7},{7,4},{8,9},{9,10},{10,1... | collective-permute-start | bytes 52232 | tf_op jit(solution)/shard_map/ppermute | solution.py:22
  456.3 88.3 %copy-start.4 = (f32[32,64,128]{2,0,1:T(8,128)S(1)}, f32[32,64,128]{2,0,1:T(8,128)}, u32[]{:S(2)}) copy-start(f32[32,64,128]{2,0,1:T(8,128)} %get-tuple-element.28) | copy-start | bytes 3145732
  456.3 88.3 %copy-start.16 = (f32[34,1,128]{2,0,1:T(8,128)S(1)}, f32[34,1,128]{2,0,1:T(8,128)}, u32[]{:S(2)}) copy-start(f32[34,1,128]{2,0,1:T(8,128)} %copy-done.14) | copy-start | bytes 52228
  (30 other events, 284.6 us)
Sparse Core Ops, SparseCore 0:
  79.2 21.9 reduce-scatter.3
  104.3 48.7 all-reduce.3
  225.8 20.6 reduce-scatter.5
  458.2 20.4 reduce-scatter.7
where the time goes:
time: 613 us; the launch traced here: 604 us
  blocking collectives  236 us (38%)
  matrix products  131 us (21%)
  waiting for transfers between devices  71.1 us (12%)
  other arithmetic  58.5 us (10%)
  local copies, waits for them, and re-layouts  54.1 us (9%)
  between operations  28.4 us (5%)
  starting transfers between devices  25.2 us (4%)
    psum x3, blocking collectives, norms_of(): lax.psum((inner(state_res, state_res, bias_res, bias_pre), inner(state_re...  124 us
    psum x2, blocking collectives, to_owners(): return lax.psum(owned, 'swath')  47.2 us
    dot_general x3, matrix products, partial_table(): table = jnp.dot(spread, inner_hot, precision=highest)  40.8 us
    psum x1, waiting for transfers between devices, to_owners(): return lax.psum(owned, 'swath')  40.4 us
    psum x1, blocking collectives, body(): lax.psum(inner(dir_state, state_out, dir_bias, bias_out), ('swath', 'chan'))  37.5 us
    mul x3, local copies, waits for them, and re-layouts, partial_table(): terms[:, None, :] * block_hot.T[None, :, :]  34.6 us
    reduce_scatter x3, waiting for transfers between devices, to_owners(): lax.psum_scatter(partial_value, 'chan', scatter_dimension=1, tiled=True)  30.6 us
    all_gather x2, blocking collectives, body(): hessian_everything = lax.all_gather(dir_bias, 'chan', axis=1, tiled=True)  27.7 us
  transfers between devices with their start and end apart: 24, of which 4 were waited for; matrix products, arithmetic and copies ran while one was open for 25% of the time, Pallas kernels for 0%

commit v1 on v0

v1 whole, which is shorter than its diff:
```python
import functools

import jax
import jax.numpy as jnp
from jax import lax
from jax.experimental import pallas as pl
from jax.experimental.pallas import tpu as pltpu
from jax.sharding import PartitionSpec as P

LEV = 128
NPRED = 8
CH_BLOCK = 256
OBS_BLOCK = 128
LAT_DEV = 32
LON_DEV = 64
ITERS = 2
LINES = 8
LANES = 128
F32 = jnp.float32
BF16 = jnp.bfloat16
NT = (((1,), (1,)), ((), ()))
VMEM_LIMIT = 60 * 1024 * 1024


def halves(value):
    high = value.astype(BF16)
    return high, (value - high.astype(F32)).astype(BF16)


def local_kernel(init, blocks, rows_ref, count_ref, cell_ref, chan_ref, prec_ref, pred_ref, jac_ref, *refs):
    if init:
        innov_ref, bp_ref, field_ref, cols_ref, table_ref, acc_ref = refs
    else:
        u_ref, coef_ref, field_ref, cols_ref, table_ref, acc_ref, split_ref, flat_ref = refs
    n_lines = cell_ref.shape[0]
    rows_tab = NPRED * blocks
    tables = 2 if init else 1
    count = count_ref[0, 0]
    field_ref[...] = jnp.zeros_like(field_ref)
    acc_ref[...] = jnp.zeros_like(acc_ref)

    if not init:
        def split_row(i, carry):
            high, low = halves(u_ref[i])
            split_ref[i] = jnp.concatenate([high, low], axis=0)
            return carry

        lax.fori_loop(0, LAT_DEV, split_row, 0)
        for b in range(blocks):
            for h in range(CH_BLOCK // LANES):
                block = coef_ref[b * (CH_BLOCK // LANES) + h]
                flat_ref[b * NPRED : (b + 1) * NPRED, h * LANES : (h + 1) * LANES] = block
        high, low = halves(flat_ref[...])
        coef2 = jnp.concatenate([high, low], axis=0)

    iota_col = lax.broadcasted_iota(jnp.int32, (LON_DEV, OBS_BLOCK), 0)
    iota_ch = lax.broadcasted_iota(jnp.int32, (CH_BLOCK, OBS_BLOCK), 0)
    iota_obs = lax.broadcasted_iota(jnp.int32, (1, OBS_BLOCK), 1)

    def step(it, carry):
        base = pl.multiple_of(it * LINES, LINES)
        cells = cell_ref[pl.ds(base, LINES), :]
        chans = chan_ref[pl.ds(base, LINES), :]
        precs = prec_ref[pl.ds(base, LINES), :]
        if init:
            innovs = innov_ref[pl.ds(base, LINES), :]
        hots, his, masks, weights, preds, jacs, rows = [], [], [], [], [], [], []
        for l in range(LINES):
            ch = chans[l : l + 1, :]
            hots.append(jnp.where(iota_ch == ch % CH_BLOCK, 1.0, 0.0).astype(BF16))
            his.append(jnp.broadcast_to(ch // CH_BLOCK, (NPRED, OBS_BLOCK)))
            masks.append(iota_col == cells[l : l + 1, :] % LON_DEV)
            slot = (base + l) * OBS_BLOCK + iota_obs
            weights.append(jnp.where(slot < count, precs[l : l + 1, :], 0.0))
            start = pl.multiple_of((base + l) * OBS_BLOCK, OBS_BLOCK)
            preds.append(pred_ref[:, pl.ds(start, OBS_BLOCK)])
            jacs.append(jac_ref[pl.ds(start, OBS_BLOCK), :])
            rows.append(rows_ref[base + l])
        values = []
        if init:
            for l in range(LINES):
                values.append(weights[l] * innovs[l : l + 1, :])
        else:
            looked = []
            for l in range(0, LINES, 2):
                pair = jnp.concatenate(hots[l : l + 2], axis=1)
                mid = jnp.dot(coef2, pair, preferred_element_type=F32)
                for j in range(2):
                    total = jnp.zeros((NPRED, OBS_BLOCK), F32)
                    lanes = slice(j * OBS_BLOCK, (j + 1) * OBS_BLOCK)
                    for b in range(blocks):
                        top = mid[b * NPRED : (b + 1) * NPRED, lanes]
                        low = mid[rows_tab + b * NPRED : rows_tab + (b + 1) * NPRED, lanes]
                        total = total + jnp.where(his[l + j] == b, top + low, 0.0)
                    looked.append(jnp.sum(total * preds[l + j], axis=0, keepdims=True))
            for l in range(LINES):
                prod = lax.dot_general(split_ref[rows[l]], jacs[l], NT, preferred_element_type=F32)
                both = prod[:LON_DEV] + prod[LON_DEV:]
                seen = jnp.sum(jnp.where(masks[l], both, 0.0), axis=0, keepdims=True)
                values.append(weights[l] * (seen + looked[l]))
        outs = []
        for l in range(LINES):
            high, low = halves(jnp.where(masks[l], values[l], 0.0))
            spread = jnp.concatenate([high, low], axis=0)
            out = jnp.dot(spread, jacs[l], preferred_element_type=F32)
            outs.append(out[:LON_DEV] + out[LON_DEV:])
        for l in range(LINES):
            field_ref[rows[l]] += outs[l]
        lefts = []
        for l in range(LINES):
            pieces = []
            terms = [preds[l] * values[l]]
            if init:
                terms.append(preds[l] * preds[l] * weights[l])
            for term in terms:
                wide = jnp.concatenate(
                    [jnp.where(his[l] == b, term, 0.0) for b in range(blocks)], axis=0
                )
                pieces.extend(halves(wide))
            lefts.append(jnp.concatenate(pieces, axis=0))
        left = jnp.concatenate(lefts, axis=1)
        hot = jnp.concatenate(hots, axis=1)
        acc_ref[...] += lax.dot_general(left, hot, NT, preferred_element_type=F32)
        return carry

    lax.fori_loop(0, n_lines // LINES, step, 0)
    per = CH_BLOCK // LANES
    used = tables * blocks * per
    for t in range(tables):
        for b in range(blocks):
            for h in range(per):
                top = t * 2 * rows_tab + b * NPRED
                low = top + rows_tab
                lanes = slice(h * LANES, (h + 1) * LANES)
                table_ref[(t * blocks + b) * per + h] = (
                    acc_ref[top : top + NPRED, lanes] + acc_ref[low : low + NPRED, lanes]
                )
    if init:
        table_ref[used : used + bp_ref.shape[0]] = bp_ref[...]
        used += bp_ref.shape[0]
    if table_ref.shape[0] > used:
        table_ref[used:] = jnp.zeros((table_ref.shape[0] - used, NPRED, LANES), F32)

    def column(i, carry):
        cols_ref[0, pl.ds(i, 1), :] = field_ref[i, 0:1, :]
        cols_ref[1, pl.ds(i, 1), :] = field_ref[i, LON_DEV - 1 : LON_DEV, :]
        return carry

    lax.fori_loop(0, LAT_DEV, column, 0)


def fold(value):
    total = value[0:8]
    for i in range(1, value.shape[0] // 8):
        total = total + value[8 * i : 8 * i + 8]
    return total


def comm_kernel(n, m, width, mode, *refs):
    refs = list(refs)
    take = lambda k: [refs.pop(0) for _ in range(k)]
    smooth_ref, g_ref, gc_ref, table_ref = take(4)
    if mode == "first":
        r_out, rc_ref, u_out, rb_out, diag_out, bp_out, pb_out, scal_out = take(8)
    else:
        p_ref, r_ref, pb_ref, rb_ref, diag_ref, bp_ref, scal_ref = take(7)
        if mode == "middle":
            u_ref, = take(1)
            r_out, rc_ref, p_out, u_out, rb_out, pb_out, scal_out = take(7)
        else:
            scal_out, = take(1)
    ta, tf, bb, s1, hu, hd, hc = take(7)
    ta_s, ta_r, h_s, h_r, s1_s, s1_r, b_s, b_r, c_s, c_r = take(10)
    if mode != "first":
        q_ref, s2, s3, s2_s, s2_r, s3_s, s3_r = take(7)
    if mode != "last":
        hu2, hd2, hc2, k_s, k_r = take(5)
    me = lax.axis_index("swath")
    z = lax.axis_index("chan")
    chunk = table_ref.shape[1]

    def to_lat(d):
        return {"swath": lax.rem(me + d, n)}

    def to_lon(d):
        return {"chan": lax.rem(z + d, m)}

    def send(src, dst, ss, rs, dev):
        copy = pltpu.make_async_remote_copy(
            src_ref=src, dst_ref=dst, send_sem=ss, recv_sem=rs,
            device_id=dev, device_id_type=pl.DeviceIdType.MESH,
        )
        copy.start()
        return copy

    barrier = pltpu.get_barrier_semaphore()
    for d in range(1, n):
        pl.semaphore_signal(barrier, inc=1, device_id=to_lat(d), device_id_type=pl.DeviceIdType.MESH)
    for d in range(1, m):
        pl.semaphore_signal(barrier, inc=1, device_id=to_lon(d), device_id_type=pl.DeviceIdType.MESH)
    pl.semaphore_wait(barrier, n - 1 + m - 1)
    pending = []

    def halo(field, cols, up, down, side, ss, rs):
        copies = [
            send(field.at[LAT_DEV - 1], up, ss.at[0], rs.at[0], to_lat(1)),
            send(field.at[0], down, ss.at[1], rs.at[1], to_lat(n - 1)),
            send(cols.at[1], side.at[0], ss.at[2], rs.at[2], to_lon(1)),
            send(cols.at[0], side.at[1], ss.at[3], rs.at[3], to_lon(m - 1)),
        ]
        pending.extend(copies)
        return copies

    def landed(copies):
        for copy in copies:
            copy.wait_recv()

    halos = halo(g_ref, gc_ref, hu, hd, hc, h_s, h_r)
    parts = [
        send(table_ref.at[lax.rem(me + d, n)], ta.at[d], ta_s.at[d], ta_r.at[d], to_lat(d))
        for d in range(1, n)
    ]
    pending.extend(parts)
    smooth = smooth_ref[0:1, :]
    top_keep = (me > 0).astype(F32)
    bottom_keep = (me < n - 1).astype(F32)
    column = lax.broadcasted_iota(jnp.int32, (LON_DEV, LEV), 0)

    def stencil(field, i, above, below, side):
        mid = field[i]
        left = jnp.where(column == 0, side[0, pl.ds(i, 1), :], pltpu.roll(mid, 1, 0))
        right = jnp.where(
            column == LON_DEV - 1, side[1, pl.ds(i, 1), :], pltpu.roll(mid, LON_DEV - 1, 0)
        )
        return mid + smooth * (above + below + left + right - 4.0 * mid)

    def sweep(field, up, down, side, use, acc):
        acc = use(0, stencil(field, 0, up[...] * top_keep, field[1], side), acc)
        acc = lax.fori_loop(
            1,
            LAT_DEV - 1,
            lambda i, a: use(i, stencil(field, i, field[i - 1], field[i + 1], side), a),
            acc,
        )
        end = LAT_DEV - 1
        return use(end, stencil(field, end, field[end - 1], down[...] * bottom_keep, side), acc)

    def keep_columns(i, row):
        rc_ref[0, pl.ds(i, 1), :] = row[0:1]
        rc_ref[1, pl.ds(i, 1), :] = row[LON_DEV - 1 : LON_DEV]

    landed(halos)
    zero = jnp.zeros((LON_DEV, LEV), F32)
    if mode == "first":

        def use(i, row, acc):
            r_out[i] = row
            keep_columns(i, row)
            return acc + row * row

    else:

        def use(i, row, acc):
            p = p_ref[i]
            q = p + row
            q_ref[i] = q
            return acc + p * q

    s1[me] = fold(sweep(g_ref, hu, hd, hc, use, zero))
    ones = [send(s1.at[me], s1.at[me], s1_s.at[d], s1_r.at[d], to_lat(d)) for d in range(1, n)]
    pending.extend(ones)
    if mode == "first":
        second = halo(r_out, rc_ref, hu2, hd2, hc2, k_s, k_r)
    landed(parts)
    total = table_ref[me]
    for d in range(1, n):
        total = total + ta[d]
    landed(ones)
    scalar = s1[0]
    for j in range(1, n):
        scalar = scalar + s1[j]
    bb[z, 0:chunk] = total
    bb[z, chunk] = scalar
    across = [send(bb.at[z], bb.at[z], b_s.at[d], b_r.at[d], to_lon(d)) for d in range(1, m)]
    pending.extend(across)
    landed(across)
    merged = bb[0]
    for j in range(1, m):
        merged = merged + bb[j]
    tf[me] = merged[0:chunk]
    state_sum = jnp.full((8, LANES), jnp.sum(merged[chunk]), F32)
    gathers = [send(tf.at[me], tf.at[me], c_s.at[d], c_r.at[d], to_lat(d)) for d in range(1, n)]
    pending.extend(gathers)
    landed(gathers)

    def tab(j):
        return tf[j // chunk, j % chunk]

    def spread(tile):
        return jnp.full((8, LANES), jnp.sum(tile), F32)

    rz_bias = jnp.zeros((8, LANES), F32)
    rr_bias = jnp.zeros((8, LANES), F32)
    if mode == "first":
        for j in range(width):
            rb = tab(j)
            bp = tab(2 * width + j)
            diag = bp + tab(width + j)
            pb = rb / diag
            rb_out[j], bp_out[j], diag_out[j], pb_out[j] = rb, bp, diag, pb
            rz_bias = rz_bias + rb * pb
            rr_bias = rr_bias + rb * rb
        scal_out[0] = state_sum + spread(rz_bias)
        scal_out[1] = state_sum + spread(rr_bias)
        scal_out[2] = jnp.zeros((8, LANES), F32)
        landed(second)

        def use_u(i, row, acc):
            u_out[i] = row
            return acc

        sweep(r_out, hu2, hd2, hc2, use_u, 0)
    else:
        curve = jnp.zeros((8, LANES), F32)
        qbs = []
        for j in range(width):
            pb = pb_ref[j]
            curve = curve + pb * (bp_ref[j] * pb + tab(j))
        alpha = scal_ref[0] / (state_sum + spread(curve))
        line = alpha[0:1, :]

        def update(i, acc):
            row = r_ref[i] - line * q_ref[i]
            if mode == "middle":
                r_out[i] = row
                keep_columns(i, row)
            return acc + row * row

        s2[me] = fold(lax.fori_loop(0, LAT_DEV, update, zero))
        twos = [send(s2.at[me], s2.at[me], s2_s.at[d], s2_r.at[d], to_lat(d)) for d in range(1, n)]
        pending.extend(twos)
        if mode == "middle":
            second = halo(r_out, rc_ref, hu2, hd2, hc2, k_s, k_r)
        for j in range(width):
            pb = pb_ref[j]
            rb = rb_ref[j] - alpha * (bp_ref[j] * pb + tab(j))
            zb = rb / diag_ref[j]
            if mode == "middle":
                rb_out[j] = rb
            rz_bias = rz_bias + rb * zb
            rr_bias = rr_bias + rb * rb
        rz_bias, rr_bias = spread(rz_bias), spread(rr_bias)
        landed(twos)
        scalar = s2[0]
        for j in range(1, n):
            scalar = scalar + s2[j]
        s3[z] = scalar
        threes = [send(s3.at[z], s3.at[z], s3_s.at[d], s3_r.at[d], to_lon(d)) for d in range(1, m)]
        pending.extend(threes)
        landed(threes)
        scalar = s3[0]
        for j in range(1, m):
            scalar = scalar + s3[j]
        state_sum = spread(scalar)
        rz_new = state_sum + rz_bias
        scal_out[0] = rz_new
        scal_out[1] = state_sum + rr_bias
        scal_out[2] = alpha
        if mode == "middle":
            beta = rz_new / scal_ref[0]
            slope = beta[0:1, :]
            for j in range(width):
                pb_out[j] = rb_out[j] / diag_ref[j] + beta * pb_ref[j]
            landed(second)

            def use_u(i, row, acc):
                u_out[i] = row + slope * u_ref[i]
                p_out[i] = r_out[i] + slope * p_ref[i]
                return acc

            sweep(r_out, hu2, hd2, hc2, use_u, 0)
    for copy in pending:
        copy.wait_send()


VM = pl.BlockSpec(memory_space=pltpu.VMEM)
SM = pl.BlockSpec(memory_space=pltpu.SMEM)


def shaped(*shape):
    return jax.ShapeDtypeStruct(shape, F32)


def body(
    innovations,
    obs_precision,
    jacobian,
    predictors,
    obs_column,
    obs_channel,
    obs_count,
    smoothing,
    bias_precision,
):
    n = lax.axis_size("swath")
    m = lax.axis_size("chan")
    me = lax.axis_index("swath")
    z = lax.axis_index("chan")
    owned_width = bias_precision.shape[1]
    own = owned_width // LANES
    width = own * m
    blocks = owned_width * m // CH_BLOCK
    slots = obs_precision.shape[0]
    lines = slots // OBS_BLOCK
    grid_lines = lambda a: a.reshape(lines, OBS_BLOCK)
    cells = grid_lines(obs_column)
    line_rows = cells[:, 0] // LON_DEV
    own_bp = bias_precision.reshape(NPRED, own, LANES).transpose(1, 0, 2)
    own_bp = jnp.where(me == 0, own_bp, 0.0)
    bp_spread = lax.dynamic_update_slice(
        jnp.zeros((width, NPRED, LANES), F32), own_bp, (z * own, 0, 0)
    )
    common = (
        line_rows, obs_count, cells, grid_lines(obs_channel), grid_lines(obs_precision),
        predictors, jacobian,
    )
    field = shaped(LAT_DEV, LON_DEV, LEV)
    cols = shaped(2, LAT_DEV, LEV)
    tab = shaped(width, NPRED, LANES)
    scal = shaped(3, 8, LANES)
    smooth = smoothing.reshape(1, LEV)

    def local(init, *extra):
        used = (3 if init else 1) * width
        padded = -(-used // n) * n
        acc_rows = (4 if init else 2) * NPRED * blocks
        scratch = [pltpu.VMEM((acc_rows, CH_BLOCK), F32)]
        if not init:
            scratch += [
                pltpu.VMEM((LAT_DEV, 2 * LON_DEV, LEV), BF16),
                pltpu.VMEM((NPRED * blocks, CH_BLOCK), F32),
            ]
        out = pl.pallas_call(
            functools.partial(local_kernel, init, blocks),
            out_shape=(field, cols, shaped(padded, NPRED, LANES)),
            in_specs=[SM, SM] + [VM] * (len(common) - 2 + len(extra)),
            out_specs=(VM, VM, VM),
            scratch_shapes=scratch,
            compiler_params=pltpu.CompilerParams(vmem_limit_bytes=VMEM_LIMIT),
            name="local_first" if init else "local_next",
        )(*common, *extra)
        return out[0], out[1], out[2].reshape(n, padded // n, NPRED, LANES)

    def comm(mode, ident, outs, table, *args):
        chunk = table.shape[1]
        sem = lambda k: [pltpu.SemaphoreType.DMA((k,)), pltpu.SemaphoreType.DMA((k,))]
        vm = lambda *s: pltpu.VMEM(s, F32)
        scratch = [
            vm(n, chunk, NPRED, LANES), vm(n, chunk, NPRED, LANES), vm(m, chunk + 1, NPRED, LANES),
            vm(n, 8, LANES), vm(LON_DEV, LEV), vm(LON_DEV, LEV), vm(2, LAT_DEV, LEV),
        ] + sem(n) + sem(4) + sem(n) + sem(m) + sem(n)
        if mode != "first":
            scratch += [vm(LAT_DEV, LON_DEV, LEV), vm(n, 8, LANES), vm(m, 8, LANES)] + sem(n) + sem(m)
        if mode != "last":
            scratch += [vm(LON_DEV, LEV), vm(LON_DEV, LEV), vm(2, LAT_DEV, LEV)] + sem(4)
        return pl.pallas_call(
            functools.partial(comm_kernel, n, m, width, mode),
            out_shape=outs,
            in_specs=[VM] * (4 + len(args)),
            out_specs=jax.tree.map(lambda _: VM, outs),
            scratch_shapes=scratch,
            compiler_params=pltpu.CompilerParams(
                collective_id=ident, has_side_effects=True, vmem_limit_bytes=VMEM_LIMIT
            ),
            name="comm_" + mode,
        )(smooth, *grads, table, *args)

    g, gc, table = local(True, grid_lines(innovations), bp_spread)
    grads = (g, gc)
    r, _, u, rb, diag, bp, pb, sc = comm(
        "first", 0, (field, cols, field, tab, tab, tab, tab, scal), table
    )
    p = r
    record = [sc[1, 0, 0]]
    state = None
    bias = None
    for turn in range(ITERS):
        g, gc, table = local(False, u, pb)
        grads = (g, gc)
        args = (p, r, pb, rb, diag, bp, sc)
        old_p, old_pb = p, pb
        if turn < ITERS - 1:
            r, _, p, u, rb, pb, sc = comm(
                "middle", 1 + turn, (field, cols, field, field, tab, tab, scal), table, *args, u
            )
        else:
            (sc,) = comm("last", 1 + turn, (scal,), table, *args)
        length = sc[2, 0, 0]
        record.append(sc[1, 0, 0])
        mine = lax.dynamic_slice(old_pb, (z * own, 0, 0), (own, NPRED, LANES))
        state = length * old_p if state is None else state + length * old_p
        bias = length * mine if bias is None else bias + length * mine
    bias = bias.transpose(1, 0, 2).reshape(NPRED, owned_width)
    return (state, bias, jnp.sqrt(jnp.stack(record)))


def solution(mesh):
    placed = (
        P(("swath", "chan")),
        P(("swath", "chan")),
        P(("swath", "chan"), None),
        P(None, ("swath", "chan")),
        P(("swath", "chan")),
        P(("swath", "chan")),
        P("swath", "chan"),
        P(),
        P(None, "chan"),
    )
    return jax.shard_map(
        body,
        mesh=mesh,
        in_specs=placed,
        out_specs=(P("swath", "chan", None), P(None, "chan"), P()),
        check_vma=False,
    )
```

time: 613 us -> 166 us (0.27); the launches traced: 604 us -> 165 us
  blocking collectives: 236 us -> 0 us
  Pallas kernels: 0 us -> 150 us
  matrix products: 131 us -> 0 us
  waiting for transfers between devices: 71.1 us -> 0 us
  other arithmetic: 58.5 us -> 9.11 us
  local copies, waits for them, and re-layouts: 54.1 us -> 4.76 us
  between operations: 28.4 us -> 1.36 us
  starting transfers between devices: 25.2 us -> 0 us
    psum x6 -> x0, blocking collectives: 208 us -> none  [the longest x3 124 us: norms_of(): lax.psum((inner(state_res, state_res, bias_res, bias_pre), inner(state_re...]
    pallas_call x0 -> x6, Pallas kernels: none -> 150 us  [the longest x3 89.9 us: comm(): pl.pallas_call(functools.partial(comm_kernel, n, m, width, mode), out_sha...]
    dot_general x15 -> x0, matrix products: 131 us -> none  [the longest x3 40.8 us: partial_table(): table = jnp.dot(spread, inner_hot, precision=highest)]
    psum x1 -> x0, waiting for transfers between devices: 40.4 us -> none  [to_owners(): return lax.psum(owned, 'swath')]
    mul x3 -> x0, local copies, waits for them, and re-layouts: 34.6 us -> none  [partial_table(): terms[:, None, :] * block_hot.T[None, :, :]]
    reduce_scatter x3 -> x0, waiting for transfers between devices: 30.6 us -> none  [to_owners(): lax.psum_scatter(partial_value, 'chan', scatter_dimension=1, tiled=True)]
    all_gather x2 -> x0, blocking collectives: 27.7 us -> none  [body(): hessian_everything = lax.all_gather(dir_bias, 'chan', axis=1, tiled=True)]
    ppermute x20 -> x0, starting transfers between devices: 25 us -> none  [the longest x10 22.6 us: with_halo(): after = lax.ppermute(leading, axis, down)]
  transfers between devices with their start and end apart: 24 -> 0, of which waited for: 4 -> 0; matrix products, arithmetic and copies ran while one was open for 25% -> 0% of each run, Pallas kernels for 0% -> 0%
where the time goes in v1:
time: 166 us; the launch traced here: 165 us
  Pallas kernels  150 us (90%)
  other arithmetic  9.11 us (5%)
  local copies, waits for them, and re-layouts  4.76 us (3%)
    pallas_call x3, Pallas kernels, comm(): pl.pallas_call(functools.partial(comm_kernel, n, m, width, mode), out_sha...  89.9 us
    pallas_call x3, Pallas kernels, local(): pl.pallas_call(functools.partial(local_kernel, init, blocks), out_shape=(...  60.3 us

profile of v1, /device:TPU:0, one launch (start us, length us, event | category | flops | bytes accessed | tf_op | source)
XLA Modules:
  0.0 165.5 jit_solution(17438444145487537279)
XLA Ops:
  0.7 0.8 bitcast_dynamic-update-slice_fusion.refs_1_
  1.5 0.0 copy-start.2
  1.5 1.0 slice_reduce_fusion
  2.4 0.5 and_select_fusion.rows_ref
  3.6 0.0 copy-done.2
  3.6 14.8 %local_first.1 = (f32[32,64,128]{2,1,0:T(8,128)}, f32[2,32,128]{2,1,0:T(8,128)}, f32[120,8,128]{2,1,0:T(8,128)}) custom-call(s32[128]{0:T(128)} %and_select_fusion.rows_ref, s32[1,1]{1,0:T(1,128)S(6)} %copy.13.count_ref, s32[128,128]{1,0:T(8,128)} %bitcast.22, s32[128,128]{1,0:T(8,128)} %bitcast.25, f32[128,128]{1,0:T(8,128)} %bitcast.28, ...), custom_call_target="tpu_custom_call" | custom-call | tf_op jit(solution)/shard_map/local_first/pallas_call | solution.py:443
  18.4 29.1 %comm_first.1 = (f32[32,64,128]{2,1,0:T(8,128)}, f32[2,32,128]{2,1,0:T(8,128)}, f32[32,64,128]{2,1,0:T(8,128)}, f32[40,8,128]{2,1,0:T(8,128)}, f32[40,8,128]{2,1...) custom-call(f32[1,128]{1,0:T(1,128)} %bitcast.35, ...), custom_call_target="tpu_custom_call" | custom-call | tf_op jit(solution)/shard_map/comm_first/pallas_call | solution.py:466
  47.6 22.7 %local_next.2 = (f32[32,64,128]{2,1,0:T(8,128)}, f32[2,32,128]{2,1,0:T(8,128)}, f32[40,8,128]{2,1,0:T(8,128)}) custom-call(s32[128]{0:T(128)} %and_select_fusion.rows_ref, s32[1,1]{1,0:T(1,128)S(6)} %copy.13.count_ref, s32[128,128]{1,0:T(8,128)} %bitcast.23, s32[128,128]{1,0:T(8,128)} %bitcast.26, f32[128,128]{1,0:T(8,128)} %bitcast.29, ...), custom_call_target="tpu_custom_call" | custom-call | tf_op jit(solution)/shard_map/local_next/pallas_call | solution.py:443
  70.3 32.5 %comm_middle.1 = (f32[32,64,128]{2,1,0:T(8,128)}, f32[2,32,128]{2,1,0:T(8,128)}, f32[32,64,128]{2,1,0:T(8,128)}, f32[32,64,128]{2,1,0:T(8,128)}, f32[40,8,128]{2...) custom-call(f32[1,128]{1,0:T(1,128)} %bitcast.36, f32[32,64,128]{2,1,0:T(8,128)} %get-tuple-element.30.refs_1_, ...), custom_call_target="tpu_custom_call" | custom-call | tf_op jit(solution)/shard_map/comm_middle/pallas_call | solution.py:466
  102.8 0.0 copy-start
  102.8 0.0 copy-start.1
  102.8 22.8 %local_next.3 = (f32[32,64,128]{2,1,0:T(8,128)}, f32[2,32,128]{2,1,0:T(8,128)}, f32[40,8,128]{2,1,0:T(8,128)}) custom-call(s32[128]{0:T(128)} %and_select_fusion.rows_ref, s32[1,1]{1,0:T(1,128)S(6)} %copy.13.count_ref, s32[128,128]{1,0:T(8,128)} %bitcast.24, s32[128,128]{1,0:T(8,128)} %bitcast.27, f32[128,128]{1,0:T(8,128)} %bitcast.30, ...), custom_call_target="tpu_custom_call" | custom-call | tf_op jit(solution)/shard_map/local_next/pallas_call | solution.py:443
  125.7 28.3 %comm_last.1 = f32[3,8,128]{2,1,0:T(8,128)} custom-call(f32[1,128]{1,0:T(1,128)} %bitcast.37, f32[32,64,128]{2,1,0:T(8,128)} %get-tuple-element.41.refs_1_, f32[2,32,128]{2,1,0:T(8,128)} %get-tuple-element.42.refs_2_, f32[8,5,8,128]{3,2,1,0:T(8,128)} %bitcast.33, f32[32,64,128]{2,1,0:T(8,128)} %get-tuple-element.44.refs_4_, ...), custom_call_target="tpu_custom_call" | custom-call | tf_op jit(solution)/shard_map/comm_last/pallas_call | solution.py:466
  153.9 1.3 fusion.1
  155.2 1.3 fusion
  156.5 1.2 slice.21
  157.7 2.5 %maximum_sqrt_fusion = f32[3]{0:T(128)} fusion(f32[1]{0:T(128)} %bitcast.16, f32[1]{0:T(128)} %bitcast.15, f32[1]{0:T(128)} %bitcast.14), kind=kLoop, calls=%fused_computation.8 | loop fusion | flops 6 | bytes 24 | tf_op jit(solution)/shard_map/sqrt | solution.py:504
  160.2 2.7 %add_bitcast_fusion = f32[8,1280]{1,0:T(8,128)} fusion(f32[40,8,128]{2,1,0:T(8,128)} %get-tuple-element.40.refs_1_.refs_6_, s32[]{:T(128)S(6)} %select_n.29, f32[40,8,128]{2,1,0:T(8,128)} %get-tuple-element.29.refs_1_.refs_6_, f32[]{:T(128)} %bitcast.11, f32[]{:T(128)} %bitcast.9), kind=kLoop, calls=%fused_computation.3 | loop fusion | flops 30720 | bytes 122892 | tf_op jit(solution)/shard_map/reshape | solution.py:503
  162.9 0.0 copy-done
  162.9 0.0 copy-done.1
  162.9 2.5 %multiply_add_fusion = f32[32,64,128]{2,1,0:T(8,128)} fusion(f32[32,64,128]{2,1,0:T(8,128)S(1)} %copy-done.1, f32[32,64,128]{2,1,0:T(8,128)S(1)} %copy-done, f32[]{:T(128)} %bitcast.11, f32[]{:T(128)} %bitcast.9), kind=kLoop, calls=%fused_computation | loop fusion | flops 786432 | bytes 3145736 | tf_op jit(solution)/shard_map/add | solution.py:501
  (1 shorter events, 0.0 us)
Async XLA Ops:
  1.5 2.2 %copy-start.2 = (f32[40,8,128]{2,1,0:T(8,128)}, f32[40,8,128]{2,1,0:T(8,128)S(1)}, u32[]{:S(2)}) copy-start(f32[40,8,128]{2,1,0:T(8,128)S(1)} %bitcast_dynamic-update-slice_fusion.refs_1_) | copy-start | bytes 491524
  102.8 60.1 %copy-start = (f32[32,64,128]{2,1,0:T(8,128)S(1)}, f32[32,64,128]{2,1,0:T(8,128)}, u32[]{:S(2)}) copy-start(f32[32,64,128]{2,1,0:T(8,128)} %get-tuple-element.33.refs_4_.refs_5_) | copy-start | bytes 3145732
  102.8 60.1 %copy-start.1 = (f32[32,64,128]{2,1,0:T(8,128)S(1)}, f32[32,64,128]{2,1,0:T(8,128)}, u32[]{:S(2)}) copy-start(f32[32,64,128]{2,1,0:T(8,128)} %get-tuple-element.44.refs_4_) | copy-start | bytes 3145732

commit v2 on v1

--- a/solution.py
+++ b/solution.py
@@ -19,7 +19,7 @@
 F32 = jnp.float32
 BF16 = jnp.bfloat16
 NT = (((1,), (1,)), ((), ()))
-VMEM_LIMIT = 60 * 1024 * 1024
+VMEM_LIMIT = 24 * 1024 * 1024
 
 
 def halves(value):
@@ -29,7 +29,7 @@
 
 def local_kernel(init, blocks, rows_ref, count_ref, cell_ref, chan_ref, prec_ref, pred_ref, jac_ref, *refs):
     if init:
-        innov_ref, bp_ref, field_ref, cols_ref, table_ref, acc_ref = refs
+        innov_ref, field_ref, cols_ref, table_ref, acc_ref = refs
     else:
         u_ref, coef_ref, field_ref, cols_ref, table_ref, acc_ref, split_ref, flat_ref = refs
     n_lines = cell_ref.shape[0]
@@ -135,9 +135,6 @@
                 table_ref[(t * blocks + b) * per + h] = (
                     acc_ref[top : top + NPRED, lanes] + acc_ref[low : low + NPRED, lanes]
                 )
-    if init:
-        table_ref[used : used + bp_ref.shape[0]] = bp_ref[...]
-        used += bp_ref.shape[0]
     if table_ref.shape[0] > used:
         table_ref[used:] = jnp.zeros((table_ref.shape[0] - used, NPRED, LANES), F32)
 
@@ -156,21 +153,25 @@
     return total
 
 
-def comm_kernel(n, m, width, mode, *refs):
+def comm_kernel(n, m, width, mode, turn, *refs):
     refs = list(refs)
     take = lambda k: [refs.pop(0) for _ in range(k)]
     smooth_ref, g_ref, gc_ref, table_ref = take(4)
     if mode == "first":
+        own_ref, = take(1)
         r_out, rc_ref, u_out, rb_out, diag_out, bp_out, pb_out, scal_out = take(8)
     else:
         p_ref, r_ref, pb_ref, rb_ref, diag_ref, bp_ref, scal_ref = take(7)
         if mode == "middle":
             u_ref, = take(1)
-            r_out, rc_ref, p_out, u_out, rb_out, pb_out, scal_out = take(7)
+            r_out, rc_ref, p_out, u_out, rb_out, pb_out, scal_out, x_out = take(8)
         else:
-            scal_out, = take(1)
-    ta, tf, bb, s1, hu, hd, hc = take(7)
-    ta_s, ta_r, h_s, h_r, s1_s, s1_r, b_s, b_r, c_s, c_r = take(10)
+            xb_ref, = take(1)
+            scal_out, norms_out, bias_out = take(3)
+    ta, tf, bb, s1, sc, hu, hd, hc = take(8)
+    ta_s, ta_r, h_s, h_r, s1_s, s1_r, b_s, b_r, c_s, c_r, sc_s, sc_r = take(12)
+    if mode == "first":
+        own_all, o_s, o_r = take(3)
     if mode != "first":
         q_ref, s2, s3, s2_s, s2_r, s3_s, s3_r = take(7)
     if mode != "last":
@@ -216,6 +217,12 @@
             copy.wait_recv()
 
     halos = halo(g_ref, gc_ref, hu, hd, hc, h_s, h_r)
+    if mode == "first":
+        own = own_ref.shape[1] // LANES
+        for j in range(own):
+            own_all[z, j] = own_ref[:, j * LANES : (j + 1) * LANES]
+        owners = [send(own_all.at[z], own_all.at[z], o_s.at[d], o_r.at[d], to_lon(d)) for d in range(1, m)]
+        pending.extend(owners)
     parts = [
         send(table_ref.at[lax.rem(me + d, n)], ta.at[d], ta_s.at[d], ta_r.at[d], to_lat(d))
         for d in range(1, n)
@@ -236,12 +243,16 @@
 
     def sweep(field, up, down, side, use, acc):
         acc = use(0, stencil(field, 0, up[...] * top_keep, field[1], side), acc)
-        acc = lax.fori_loop(
-            1,
-            LAT_DEV - 1,
-            lambda i, a: use(i, stencil(field, i, field[i - 1], field[i + 1], side), a),
-            acc,
-        )
+        inner = LAT_DEV - 2
+        group = next(k for k in (5, 4, 3, 2, 1) if inner % k == 0)
+
+        def rows(it, a):
+            for k in range(group):
+                i = 1 + it * group + k
+                a = use(i, stencil(field, i, field[i - 1], field[i + 1], side), a)
+            return a
+
+        acc = lax.fori_loop(0, inner // group, rows, acc)
         end = LAT_DEV - 1
         return use(end, stencil(field, end, field[end - 1], down[...] * bottom_keep, side), acc)
 
@@ -249,7 +260,6 @@
         rc_ref[0, pl.ds(i, 1), :] = row[0:1]
         rc_ref[1, pl.ds(i, 1), :] = row[LON_DEV - 1 : LON_DEV]
 
-    landed(halos)
     zero = jnp.zeros((LON_DEV, LEV), F32)
     if mode == "first":
 
@@ -266,31 +276,45 @@
             q_ref[i] = q
             return acc + p * q
 
-    s1[me] = fold(sweep(g_ref, hu, hd, hc, use, zero))
-    ones = [send(s1.at[me], s1.at[me], s1_s.at[d], s1_r.at[d], to_lat(d)) for d in range(1, n)]
-    pending.extend(ones)
+    def scatter_sum():
+        landed(parts)
+        total = table_ref[me]
+        for d in range(1, n):
+            total = total + ta[d]
+        bb[z] = total
+        across = [send(bb.at[z], bb.at[z], b_s.at[d], b_r.at[d], to_lon(d)) for d in range(1, m)]
+        pending.extend(across)
+        return across
+
+    def everywhere(buf, tile, ss, rs):
+        buf[me] = tile
+        copies = [send(buf.at[me], buf.at[me], ss.at[d], rs.at[d], to_lat(d)) for d in range(1, n)]
+        pending.extend(copies)
+        return copies
+
+    def summed(buf, count):
+        total = buf[0]
+        for j in range(1, count):
+            total = total + buf[j]
+        return total
+
+    def along_lon(buf, tile, ss, rs):
+        buf[z] = tile
+        copies = [send(buf.at[z], buf.at[z], ss.at[d], rs.at[d], to_lon(d)) for d in range(1, m)]
+        pending.extend(copies)
+        return copies
+
+    if mode != "first":
+        across = scatter_sum()
+    landed(halos)
+    ones = everywhere(s1, fold(sweep(g_ref, hu, hd, hc, use, zero)), s1_s, s1_r)
     if mode == "first":
         second = halo(r_out, rc_ref, hu2, hd2, hc2, k_s, k_r)
-    landed(parts)
-    total = table_ref[me]
-    for d in range(1, n):
-        total = total + ta[d]
+        across = scatter_sum()
+    landed(across)
+    gathers = everywhere(tf, summed(bb, m), c_s, c_r)
     landed(ones)
-    scalar = s1[0]
-    for j in range(1, n):
-        scalar = scalar + s1[j]
-    bb[z, 0:chunk] = total
-    bb[z, chunk] = scalar
-    across = [send(bb.at[z], bb.at[z], b_s.at[d], b_r.at[d], to_lon(d)) for d in range(1, m)]
-    pending.extend(across)
-    landed(across)
-    merged = bb[0]
-    for j in range(1, m):
-        merged = merged + bb[j]
-    tf[me] = merged[0:chunk]
-    state_sum = jnp.full((8, LANES), jnp.sum(merged[chunk]), F32)
-    gathers = [send(tf.at[me], tf.at[me], c_s.at[d], c_r.at[d], to_lat(d)) for d in range(1, n)]
-    pending.extend(gathers)
+    crossing = along_lon(sc, summed(s1, n), sc_s, sc_r)
     landed(gathers)
 
     def tab(j):
@@ -302,17 +326,21 @@
     rz_bias = jnp.zeros((8, LANES), F32)
     rr_bias = jnp.zeros((8, LANES), F32)
     if mode == "first":
+        landed(owners)
         for j in range(width):
             rb = tab(j)
-            bp = tab(2 * width + j)
+            bp = own_all[j // own, j % own]
             diag = bp + tab(width + j)
             pb = rb / diag
             rb_out[j], bp_out[j], diag_out[j], pb_out[j] = rb, bp, diag, pb
             rz_bias = rz_bias + rb * pb
             rr_bias = rr_bias + rb * rb
-        scal_out[0] = state_sum + spread(rz_bias)
-        scal_out[1] = state_sum + spread(rr_bias)
-        scal_out[2] = jnp.zeros((8, LANES), F32)
+        rz_bias, rr_bias = spread(rz_bias), spread(rr_bias)
+        landed(crossing)
+        state_sum = spread(summed(sc, m))
+        scal_out[...] = jnp.zeros(scal_out.shape, F32)
+        scal_out[0] = state_sum + rz_bias
+        scal_out[1] = state_sum + rr_bias
         landed(second)
 
         def use_u(i, row, acc):
@@ -322,23 +350,25 @@
         sweep(r_out, hu2, hd2, hc2, use_u, 0)
     else:
         curve = jnp.zeros((8, LANES), F32)
-        qbs = []
         for j in range(width):
             pb = pb_ref[j]
             curve = curve + pb * (bp_ref[j] * pb + tab(j))
-        alpha = scal_ref[0] / (state_sum + spread(curve))
+        curve = spread(curve)
+        landed(crossing)
+        alpha = scal_ref[0] / (spread(summed(sc, m)) + curve)
         line = alpha[0:1, :]
 
-        def update(i, acc):
-            row = r_ref[i] - line * q_ref[i]
-            if mode == "middle":
-                r_out[i] = row
-                keep_columns(i, row)
-            return acc + row * row
-
-        s2[me] = fold(lax.fori_loop(0, LAT_DEV, update, zero))
-        twos = [send(s2.at[me], s2.at[me], s2_s.at[d], s2_r.at[d], to_lat(d)) for d in range(1, n)]
-        pending.extend(twos)
+        def update(it, acc):
+            for k in range(4):
+                i = it * 4 + k
+                row = r_ref[i] - line * q_ref[i]
+                if mode == "middle":
+                    r_out[i] = row
+                    keep_columns(i, row)
+                acc = acc + row * row
+            return acc
+
+        twos = everywhere(s2, fold(lax.fori_loop(0, LAT_DEV // 4, update, zero)), s2_s, s2_r)
         if mode == "middle":
             second = halo(r_out, rc_ref, hu2, hd2, hc2, k_s, k_r)
         for j in range(width):
@@ -347,25 +377,31 @@
             zb = rb / diag_ref[j]
             if mode == "middle":
                 rb_out[j] = rb
+                x_out[j] = alpha * pb
             rz_bias = rz_bias + rb * zb
             rr_bias = rr_bias + rb * rb
         rz_bias, rr_bias = spread(rz_bias), spread(rr_bias)
         landed(twos)
-        scalar = s2[0]
-        for j in range(1, n):
-            scalar = scalar + s2[j]
-        s3[z] = scalar
-        threes = [send(s3.at[z], s3.at[z], s3_s.at[d], s3_r.at[d], to_lon(d)) for d in range(1, m)]
-        pending.extend(threes)
+        threes = along_lon(s3, summed(s2, n), s3_s, s3_r)
+        if mode == "last":
+            own = bias_out.shape[1] // LANES
+            for j in range(own):
+                bias_out[:, j * LANES : (j + 1) * LANES] = (
+                    xb_ref[z * own + j] + alpha * pb_ref[z * own + j]
+                )
         landed(threes)
-        scalar = s3[0]
-        for j in range(1, m):
-            scalar = scalar + s3[j]
-        state_sum = spread(scalar)
+        state_sum = spread(summed(s3, m))
         rz_new = state_sum + rz_bias
+        scal_out[...] = scal_ref[...]
         scal_out[0] = rz_new
-        scal_out[1] = state_sum + rr_bias
-        scal_out[2] = alpha
+        scal_out[1 + turn] = state_sum + rr_bias
+        scal_out[1 + ITERS + turn] = alpha
+        if mode == "last":
+            lane = lax.broadcasted_iota(jnp.int32, (8, LANES), 1)
+            norms = jnp.zeros((8, LANES), F32)
+            for j in range(ITERS + 1):
+                norms = jnp.where(lane == j, scal_out[1 + j], norms)
+            norms_out[...] = jnp.sqrt(norms)
         if mode == "middle":
             beta = rz_new / scal_ref[0]
             slope = beta[0:1, :]
@@ -404,8 +440,6 @@
 ):
     n = lax.axis_size("swath")
     m = lax.axis_size("chan")
-    me = lax.axis_index("swath")
-    z = lax.axis_index("chan")
     owned_width = bias_precision.shape[1]
     own = owned_width // LANES
     width = own * m
@@ -415,11 +449,6 @@
     grid_lines = lambda a: a.reshape(lines, OBS_BLOCK)
     cells = grid_lines(obs_column)
     line_rows = cells[:, 0] // LON_DEV
-    own_bp = bias_precision.reshape(NPRED, own, LANES).transpose(1, 0, 2)
-    own_bp = jnp.where(me == 0, own_bp, 0.0)
-    bp_spread = lax.dynamic_update_slice(
-        jnp.zeros((width, NPRED, LANES), F32), own_bp, (z * own, 0, 0)
-    )
     common = (
         line_rows, obs_count, cells, grid_lines(obs_channel), grid_lines(obs_precision),
         predictors, jacobian,
@@ -427,11 +456,11 @@
     field = shaped(LAT_DEV, LON_DEV, LEV)
     cols = shaped(2, LAT_DEV, LEV)
     tab = shaped(width, NPRED, LANES)
-    scal = shaped(3, 8, LANES)
+    scal = shaped(2 + 2 * ITERS, 8, LANES)
     smooth = smoothing.reshape(1, LEV)
 
     def local(init, *extra):
-        used = (3 if init else 1) * width
+        used = (2 if init else 1) * width
         padded = -(-used // n) * n
         acc_rows = (4 if init else 2) * NPRED * blocks
         scratch = [pltpu.VMEM((acc_rows, CH_BLOCK), F32)]
@@ -456,15 +485,17 @@
         sem = lambda k: [pltpu.SemaphoreType.DMA((k,)), pltpu.SemaphoreType.DMA((k,))]
         vm = lambda *s: pltpu.VMEM(s, F32)
         scratch = [
-            vm(n, chunk, NPRED, LANES), vm(n, chunk, NPRED, LANES), vm(m, chunk + 1, NPRED, LANES),
-            vm(n, 8, LANES), vm(LON_DEV, LEV), vm(LON_DEV, LEV), vm(2, LAT_DEV, LEV),
-        ] + sem(n) + sem(4) + sem(n) + sem(m) + sem(n)
+            vm(n, chunk, NPRED, LANES), vm(n, chunk, NPRED, LANES), vm(m, chunk, NPRED, LANES),
+            vm(n, 8, LANES), vm(m, 8, LANES), vm(LON_DEV, LEV), vm(LON_DEV, LEV), vm(2, LAT_DEV, LEV),
+        ] + sem(n) + sem(4) + sem(n) + sem(m) + sem(n) + sem(m)
+        if mode == "first":
+            scratch += [vm(m, own, NPRED, LANES)] + sem(m)
         if mode != "first":
             scratch += [vm(LAT_DEV, LON_DEV, LEV), vm(n, 8, LANES), vm(m, 8, LANES)] + sem(n) + sem(m)
         if mode != "last":
             scratch += [vm(LON_DEV, LEV), vm(LON_DEV, LEV), vm(2, LAT_DEV, LEV)] + sem(4)
         return pl.pallas_call(
-            functools.partial(comm_kernel, n, m, width, mode),
+            functools.partial(comm_kernel, n, m, width, mode, ident),
             out_shape=outs,
             in_specs=[VM] * (4 + len(args)),
             out_specs=jax.tree.map(lambda _: VM, outs),
@@ -475,33 +506,28 @@
             name="comm_" + mode,
         )(smooth, *grads, table, *args)
 
-    g, gc, table = local(True, grid_lines(innovations), bp_spread)
+    g, gc, table = local(True, grid_lines(innovations))
     grads = (g, gc)
     r, _, u, rb, diag, bp, pb, sc = comm(
-        "first", 0, (field, cols, field, tab, tab, tab, tab, scal), table
+        "first", 0, (field, cols, field, tab, tab, tab, tab, scal), table, bias_precision
     )
     p = r
-    record = [sc[1, 0, 0]]
     state = None
-    bias = None
-    for turn in range(ITERS):
+    total = None
+    for turn in range(1, ITERS + 1):
         g, gc, table = local(False, u, pb)
         grads = (g, gc)
         args = (p, r, pb, rb, diag, bp, sc)
-        old_p, old_pb = p, pb
-        if turn < ITERS - 1:
-            r, _, p, u, rb, pb, sc = comm(
-                "middle", 1 + turn, (field, cols, field, field, tab, tab, scal), table, *args, u
-            )
+        old_p = p
+        if turn < ITERS:
+            outs = (field, cols, field, field, tab, tab, scal, tab)
+            r, _, p, u, rb, pb, sc, total = comm("middle", turn, outs, table, *args, u)
         else:
-            (sc,) = comm("last", 1 + turn, (scal,), table, *args)
-        length = sc[2, 0, 0]
-        record.append(sc[1, 0, 0])
-        mine = lax.dynamic_slice(old_pb, (z * own, 0, 0), (own, NPRED, LANES))
+            outs = (scal, shaped(8, LANES), shaped(NPRED, owned_width))
+            sc, norms, bias = comm("last", turn, outs, table, *args, total)
+        length = sc[1 + ITERS + turn, 0]
         state = length * old_p if state is None else state + length * old_p
-        bias = length * mine if bias is None else bias + length * mine
-    bias = bias.transpose(1, 0, 2).reshape(NPRED, owned_width)
-    return (state, bias, jnp.sqrt(jnp.stack(record)))
+    return (state, bias, norms[0, : ITERS + 1])
 
 
 def solution(mesh):

time: 166 us -> 133 us (0.80)
  Pallas kernels: 150 us -> 121 us
  other arithmetic: 9.11 us -> 1.16 us
  local copies, waits for them, and re-layouts: 4.76 us -> 8.68 us
    pallas_call x3, Pallas kernels: 89.9 us -> 70.5 us  [comm(): pl.pallas_call(functools.partial(comm_kernel, n, m, width, mode, ident),...]
    pallas_call x3, Pallas kernels: 60.3 us -> 50.7 us  [local(): pl.pallas_call(functools.partial(local_kernel, init, blocks), out_shape=(...]
    unnamed x6 -> x23, local copies, waits for them, and re-layouts: 0.01 us -> 7.22 us
    slice x3 -> x0, local copies, waits for them, and re-layouts: 3.75 us -> none  [the longest x2 2.54 us: body(): record.append(sc[1, 0, 0])]
    reshape x1 -> x0, other arithmetic: 2.73 us -> none  [body(): bias = bias.transpose(1, 0, 2).reshape(NPRED, owned_width)]
    sqrt x1 -> x0, other arithmetic: 2.52 us -> none  [body(): return (state, bias, jnp.sqrt(jnp.stack(record)))]
where the time goes in v2:
time: 133 us; the launch traced here: 132 us
  Pallas kernels  121 us (91%)
  local copies, waits for them, and re-layouts  8.68 us (7%)
  between operations  1.45 us (1%)
    pallas_call x3, Pallas kernels, comm(): pl.pallas_call(functools.partial(comm_kernel, n, m, width, mode, ident),...  70.5 us
    pallas_call x3, Pallas kernels, local(): pl.pallas_call(functools.partial(local_kernel, init, blocks), out_shape=(...  50.7 us
    unnamed x23, local copies, waits for them, and re-layouts  7.22 us

profile of v2, /device:TPU:0, one launch (start us, length us, event | category | flops | bytes accessed | tf_op | source)
XLA Modules:
  0.0 132.4 jit_solution(6603851184147395193)
XLA Ops:
  0.6 0.0 copy-start.10
  0.6 0.0 copy-start.5
  1.3 0.9 slice_reduce_fusion
  2.3 0.0 copy-start
  2.3 2.2 %copy-done = bf16[16384,128]{1,0:T(8,128)(2,1)S(1)} copy-done((bf16[16384,128]{1,0:T(8,128)(2,1)S(1)}, bf16[16384,128]{1,0:T(8,128)(2,1)}, u32[]{:S(2)}) %copy-start) | copy-done | bytes 4194328
  4.5 0.0 copy-start.2
  4.5 1.0 copy-done.2
  5.5 0.0 copy-start.4
  5.5 0.8 copy-done.4
  6.4 0.0 copy-start.6
  6.4 0.8 copy-done.6
  7.2 0.0 copy-start.7
  7.2 0.8 copy-done.7
  8.1 0.0 copy-start.8
  8.1 0.8 copy-done.8
  8.9 0.0 copy-start.9
  8.9 0.0 copy-start.1
  8.9 0.0 copy-start.3
  8.9 11.6 %local_first.1 = (f32[32,64,128]{2,1,0:T(8,128)S(1)}, f32[2,32,128]{2,1,0:T(8,128)S(1)}, f32[80,8,128]{2,1,0:T(8,128)S(1)}) custom-call(s32[128]{0:T(128)S(1)} %and_select_fusion.rows_ref, s32[1,1]{1,0:T(1,128)S(6)} %copy.13.count_ref, s32[128,128]{1,0:T(8,128)S(1)} %bitcast.15, s32[128,128]{1,0:T(8,128)S(1)} %bitcast.18, f32[128,128]{1,0:T(8,128)S(1)} %bitcast.21, ...), custom_call_target="tpu_custom_call" | custom-call | tf_op jit(solution)/shard_map/local_first/pallas_call | solution.py:472
  20.5 0.0 copy-done.10
  20.5 0.0 copy-done.9
  20.6 23.5 %comm_first.1 = (f32[32,64,128]{2,1,0:T(8,128)S(1)}, f32[2,32,128]{2,1,0:T(8,128)}, f32[32,64,128]{2,1,0:T(8,128)S(1)}, f32[40,8,128]{2,1,0:T(8,128)S(1)}, f32[4...) custom-call(f32[1,128]{1,0:T(1,128)S(1)} %bitcast.28, ...), custom_call_target="tpu_custom_call" | custom-call | tf_op jit(solution)/shard_map/comm_first/pallas_call | solution.py:497
  44.1 0.0 copy-done.5
  44.1 0.0 copy-done.1
  44.1 0.0 copy-done.3
  44.1 19.5 %local_next.2 = (f32[32,64,128]{2,1,0:T(8,128)S(1)}, f32[2,32,128]{2,1,0:T(8,128)S(1)}, f32[40,8,128]{2,1,0:T(8,128)S(1)}) custom-call(s32[128]{0:T(128)S(1)} %and_select_fusion.rows_ref, s32[1,1]{1,0:T(1,128)S(6)} %copy.13.count_ref, s32[128,128]{1,0:T(8,128)S(1)} %bitcast.16, s32[128,128]{1,0:T(8,128)S(1)} %bitcast.19, f32[128,128]{1,0:T(8,128)S(1)} %bitcast.22, ...), custom_call_target="tpu_custom_call" | custom-call | tf_op jit(solution)/shard_map/local_next/pallas_call | solution.py:472
  63.7 25.2 %comm_middle.1 = (f32[32,64,128]{2,1,0:T(8,128)S(1)}, f32[2,32,128]{2,1,0:T(8,128)}, f32[32,64,128]{2,1,0:T(8,128)S(1)}, f32[32,64,128]{2,1,0:T(8,128)S(1)}, f32...) custom-call(f32[1,128]{1,0:T(1,128)S(1)} %bitcast.29, ...), custom_call_target="tpu_custom_call" | custom-call | tf_op jit(solution)/shard_map/comm_middle/pallas_call | solution.py:497
  88.8 19.5 %local_next.3 = (f32[32,64,128]{2,1,0:T(8,128)S(1)}, f32[2,32,128]{2,1,0:T(8,128)S(1)}, f32[40,8,128]{2,1,0:T(8,128)S(1)}) custom-call(s32[128]{0:T(128)S(1)} %and_select_fusion.rows_ref, s32[1,1]{1,0:T(1,128)S(6)} %copy.13.count_ref, s32[128,128]{1,0:T(8,128)S(1)} %bitcast.17, s32[128,128]{1,0:T(8,128)S(1)} %bitcast.20, f32[128,128]{1,0:T(8,128)S(1)} %bitcast.23, ...), custom_call_target="tpu_custom_call" | custom-call | tf_op jit(solution)/shard_map/local_next/pallas_call | solution.py:472
  108.4 21.8 %comm_last.1 = (f32[6,8,128]{2,1,0:T(8,128)S(1)}, f32[8,128]{1,0:T(8,128)S(1)}, f32[8,1280]{1,0:T(8,128)S(1)}) custom-call(f32[1,128]{1,0:T(1,128)S(1)} %bitcast.30, f32[32,64,128]{2,1,0:T(8,128)S(1)} %get-tuple-element.45.refs_1_, f32[2,32,128]{2,1,0:T(8,128)S(1)} %get-tuple-element.46.refs_2_, f32[8,5,8,128]{3,2,1,0:T(8,128)S(1)} %bitcast.25, ...), custom_call_target="tpu_custom_call" | custom-call | tf_op jit(solution)/shard_map/comm_last/pallas_call | solution.py:497
  130.1 1.2 multiply_add_fusion
  131.3 0.5 slice_bitcast_fusion
  131.8 0.6 copy.14
  (2 shorter events, 0.0 us)
Async XLA Ops:
  0.6 19.9 %copy-start.10 = (f32[128]{0:T(128)S(1)}, f32[128]{0:T(128)}, u32[]{:S(2)}) copy-start(f32[128]{0:T(128)} %param.16) | copy-start | bytes 1540
  0.6 43.5 %copy-start.5 = (s32[16384]{0:T(1024)S(1)}, s32[16384]{0:T(1024)}, u32[]{:S(2)}) copy-start(s32[16384]{0:T(1024)} %param.13) | copy-start | bytes 196612
  2.3 2.2 %copy-start = (bf16[16384,128]{1,0:T(8,128)(2,1)S(1)}, bf16[16384,128]{1,0:T(8,128)(2,1)}, u32[]{:S(2)}) copy-start(bf16[16384,128]{1,0:T(8,128)(2,1)} %jac_ref.5) | copy-start | bytes 12582916
  4.5 1.0 copy-start.2
  5.5 0.8 copy-start.4
  6.4 0.8 copy-start.6
  7.2 0.8 copy-start.7
  8.1 0.8 copy-start.8
  8.9 11.7 %copy-start.9 = (f32[8,1280]{1,0:T(8,128)S(1)}, f32[8,1280]{1,0:T(8,128)}, u32[]{:S(2)}) copy-start(f32[8,1280]{1,0:T(8,128)} %refs_4_.1) | copy-start | bytes 122884
  8.9 35.2 %copy-start.1 = (bf16[16384,128]{1,0:T(8,128)(2,1)S(1)}, bf16[16384,128]{1,0:T(8,128)(2,1)}, u32[]{:S(2)}) copy-start(bf16[16384,128]{1,0:T(8,128)(2,1)} %jac_ref.5) | copy-start | bytes 12582916
  8.9 35.2 %copy-start.3 = (f32[8,16384]{1,0:T(8,128)S(1)}, f32[8,16384]{1,0:T(8,128)}, u32[]{:S(2)}) copy-start(f32[8,16384]{1,0:T(8,128)} %pred_ref.5) | copy-start | bytes 1572868

commit v3 on v2

--- a/solution.py
+++ b/solution.py
@@ -42,7 +42,7 @@
     if not init:
         def split_row(i, carry):
             high, low = halves(u_ref[i])
-            split_ref[i] = jnp.concatenate([high, low], axis=0)
+            split_ref[i] = jnp.concatenate([high, low], axis=1)
             return carry
 
         lax.fori_loop(0, LAT_DEV, split_row, 0)
@@ -51,7 +51,7 @@
                 block = coef_ref[b * (CH_BLOCK // LANES) + h]
                 flat_ref[b * NPRED : (b + 1) * NPRED, h * LANES : (h + 1) * LANES] = block
         high, low = halves(flat_ref[...])
-        coef2 = jnp.concatenate([high, low], axis=0)
+        coef2 = jnp.concatenate([high, low], axis=1)
 
     iota_col = lax.broadcasted_iota(jnp.int32, (LON_DEV, OBS_BLOCK), 0)
     iota_ch = lax.broadcasted_iota(jnp.int32, (CH_BLOCK, OBS_BLOCK), 0)
@@ -84,31 +84,32 @@
             looked = []
             for l in range(0, LINES, 2):
                 pair = jnp.concatenate(hots[l : l + 2], axis=1)
-                mid = jnp.dot(coef2, pair, preferred_element_type=F32)
+                mid = jnp.dot(
+                    coef2, jnp.concatenate([pair, pair], axis=0), preferred_element_type=F32
+                )
                 for j in range(2):
                     total = jnp.zeros((NPRED, OBS_BLOCK), F32)
                     lanes = slice(j * OBS_BLOCK, (j + 1) * OBS_BLOCK)
                     for b in range(blocks):
                         top = mid[b * NPRED : (b + 1) * NPRED, lanes]
-                        low = mid[rows_tab + b * NPRED : rows_tab + (b + 1) * NPRED, lanes]
-                        total = total + jnp.where(his[l + j] == b, top + low, 0.0)
+                        total = total + jnp.where(his[l + j] == b, top, 0.0)
                     looked.append(jnp.sum(total * preds[l + j], axis=0, keepdims=True))
             for l in range(LINES):
-                prod = lax.dot_general(split_ref[rows[l]], jacs[l], NT, preferred_element_type=F32)
-                both = prod[:LON_DEV] + prod[LON_DEV:]
+                twice = jnp.concatenate([jacs[l], jacs[l]], axis=1)
+                both = lax.dot_general(split_ref[rows[l]], twice, NT, preferred_element_type=F32)
                 seen = jnp.sum(jnp.where(masks[l], both, 0.0), axis=0, keepdims=True)
                 values.append(weights[l] * (seen + looked[l]))
         outs = []
         for l in range(LINES):
             high, low = halves(jnp.where(masks[l], values[l], 0.0))
-            spread = jnp.concatenate([high, low], axis=0)
-            out = jnp.dot(spread, jacs[l], preferred_element_type=F32)
-            outs.append(out[:LON_DEV] + out[LON_DEV:])
+            spread = jnp.concatenate([high, low], axis=1)
+            twice = jnp.concatenate([jacs[l], jacs[l]], axis=0)
+            outs.append(jnp.dot(spread, twice, preferred_element_type=F32))
         for l in range(LINES):
             field_ref[rows[l]] += outs[l]
-        lefts = []
+        lefts, rights = [], []
         for l in range(LINES):
-            pieces = []
+            highs, lows = [], []
             terms = [preds[l] * values[l]]
             if init:
                 terms.append(preds[l] * preds[l] * weights[l])
@@ -116,10 +117,13 @@
                 wide = jnp.concatenate(
                     [jnp.where(his[l] == b, term, 0.0) for b in range(blocks)], axis=0
                 )
-                pieces.extend(halves(wide))
-            lefts.append(jnp.concatenate(pieces, axis=0))
-        left = jnp.concatenate(lefts, axis=1)
-        hot = jnp.concatenate(hots, axis=1)
+                high, low = halves(wide)
+                highs.append(high)
+                lows.append(low)
+            lefts.append(jnp.concatenate(highs, axis=0))
+            rights.append(jnp.concatenate(lows, axis=0))
+        left = jnp.concatenate(lefts + rights, axis=1)
+        hot = jnp.concatenate(hots + hots, axis=1)
         acc_ref[...] += lax.dot_general(left, hot, NT, preferred_element_type=F32)
         return carry
 
@@ -129,12 +133,9 @@
     for t in range(tables):
         for b in range(blocks):
             for h in range(per):
-                top = t * 2 * rows_tab + b * NPRED
-                low = top + rows_tab
+                top = t * rows_tab + b * NPRED
                 lanes = slice(h * LANES, (h + 1) * LANES)
-                table_ref[(t * blocks + b) * per + h] = (
-                    acc_ref[top : top + NPRED, lanes] + acc_ref[low : low + NPRED, lanes]
-                )
+                table_ref[(t * blocks + b) * per + h] = acc_ref[top : top + NPRED, lanes]
     if table_ref.shape[0] > used:
         table_ref[used:] = jnp.zeros((table_ref.shape[0] - used, NPRED, LANES), F32)
 
@@ -462,11 +463,11 @@
     def local(init, *extra):
         used = (2 if init else 1) * width
         padded = -(-used // n) * n
-        acc_rows = (4 if init else 2) * NPRED * blocks
+        acc_rows = (2 if init else 1) * NPRED * blocks
         scratch = [pltpu.VMEM((acc_rows, CH_BLOCK), F32)]
         if not init:
             scratch += [
-                pltpu.VMEM((LAT_DEV, 2 * LON_DEV, LEV), BF16),
+                pltpu.VMEM((LAT_DEV, LON_DEV, 2 * LEV), BF16),
                 pltpu.VMEM((NPRED * blocks, CH_BLOCK), F32),
             ]
         out = pl.pallas_call(

time: 133 us -> 131 us (0.985)
  Pallas kernels: 121 us -> 119 us
    pallas_call x3, Pallas kernels: 50.7 us -> 48.3 us  [local(): pl.pallas_call(functools.partial(local_kernel, init, blocks), out_shape=(...]
where the time goes in v3:
time: 131 us; the launch traced here: 130 us
  Pallas kernels  119 us (91%)
  local copies, waits for them, and re-layouts  8.68 us (7%)
  between operations  1.45 us (1%)
    pallas_call x3, Pallas kernels, comm(): pl.pallas_call(functools.partial(comm_kernel, n, m, width, mode, ident),...  70.5 us
    pallas_call x3, Pallas kernels, local(): pl.pallas_call(functools.partial(local_kernel, init, blocks), out_shape=(...  48.3 us
    unnamed x23, local copies, waits for them, and re-layouts  7.22 us

profile of v3, /device:TPU:0, one launch (start us, length us, event | category | flops | bytes accessed | tf_op | source)
XLA Modules:
  0.0 130.1 jit_solution(2013120723297214589)
XLA Ops:
  0.6 0.0 copy-start.10
  0.6 0.0 copy-start.5
  1.3 0.9 slice_reduce_fusion
  2.3 0.0 copy-start
  2.3 2.2 %copy-done = bf16[16384,128]{1,0:T(8,128)(2,1)S(1)} copy-done((bf16[16384,128]{1,0:T(8,128)(2,1)S(1)}, bf16[16384,128]{1,0:T(8,128)(2,1)}, u32[]{:S(2)}) %copy-start) | copy-done | bytes 4194328
  4.5 0.0 copy-start.2
  4.5 1.0 copy-done.2
  5.5 0.0 copy-start.4
  5.5 0.8 copy-done.4
  6.4 0.0 copy-start.6
  6.4 0.8 copy-done.6
  7.2 0.0 copy-start.7
  7.2 0.8 copy-done.7
  8.1 0.0 copy-start.8
  8.1 0.8 copy-done.8
  8.9 0.0 copy-start.9
  8.9 0.0 copy-start.1
  8.9 0.0 copy-start.3
  8.9 11.3 %local_first.1 = (f32[32,64,128]{2,1,0:T(8,128)S(1)}, f32[2,32,128]{2,1,0:T(8,128)S(1)}, f32[80,8,128]{2,1,0:T(8,128)S(1)}) custom-call(s32[128]{0:T(128)S(1)} %and_select_fusion.rows_ref, s32[1,1]{1,0:T(1,128)S(6)} %copy.13.count_ref, s32[128,128]{1,0:T(8,128)S(1)} %bitcast.15, s32[128,128]{1,0:T(8,128)S(1)} %bitcast.18, f32[128,128]{1,0:T(8,128)S(1)} %bitcast.21, ...), custom_call_target="tpu_custom_call" | custom-call | tf_op jit(solution)/shard_map/local_first/pallas_call | solution.py:473
  20.2 0.0 copy-done.10
  20.2 0.0 copy-done.9
  20.2 23.5 %comm_first.1 = (f32[32,64,128]{2,1,0:T(8,128)S(1)}, f32[2,32,128]{2,1,0:T(8,128)}, f32[32,64,128]{2,1,0:T(8,128)S(1)}, f32[40,8,128]{2,1,0:T(8,128)S(1)}, f32[4...) custom-call(f32[1,128]{1,0:T(1,128)S(1)} %bitcast.28, ...), custom_call_target="tpu_custom_call" | custom-call | tf_op jit(solution)/shard_map/comm_first/pallas_call | solution.py:498
  43.8 0.0 copy-done.5
  43.8 0.0 copy-done.1
  43.8 0.0 copy-done.3
  43.8 18.5 %local_next.2 = (f32[32,64,128]{2,1,0:T(8,128)S(1)}, f32[2,32,128]{2,1,0:T(8,128)S(1)}, f32[40,8,128]{2,1,0:T(8,128)S(1)}) custom-call(s32[128]{0:T(128)S(1)} %and_select_fusion.rows_ref, s32[1,1]{1,0:T(1,128)S(6)} %copy.13.count_ref, s32[128,128]{1,0:T(8,128)S(1)} %bitcast.16, s32[128,128]{1,0:T(8,128)S(1)} %bitcast.19, f32[128,128]{1,0:T(8,128)S(1)} %bitcast.22, ...), custom_call_target="tpu_custom_call" | custom-call | tf_op jit(solution)/shard_map/local_next/pallas_call | solution.py:473
  62.3 25.2 %comm_middle.1 = (f32[32,64,128]{2,1,0:T(8,128)S(1)}, f32[2,32,128]{2,1,0:T(8,128)}, f32[32,64,128]{2,1,0:T(8,128)S(1)}, f32[32,64,128]{2,1,0:T(8,128)S(1)}, f32...) custom-call(f32[1,128]{1,0:T(1,128)S(1)} %bitcast.29, ...), custom_call_target="tpu_custom_call" | custom-call | tf_op jit(solution)/shard_map/comm_middle/pallas_call | solution.py:498
  87.5 18.5 %local_next.3 = (f32[32,64,128]{2,1,0:T(8,128)S(1)}, f32[2,32,128]{2,1,0:T(8,128)S(1)}, f32[40,8,128]{2,1,0:T(8,128)S(1)}) custom-call(s32[128]{0:T(128)S(1)} %and_select_fusion.rows_ref, s32[1,1]{1,0:T(1,128)S(6)} %copy.13.count_ref, s32[128,128]{1,0:T(8,128)S(1)} %bitcast.17, s32[128,128]{1,0:T(8,128)S(1)} %bitcast.20, f32[128,128]{1,0:T(8,128)S(1)} %bitcast.23, ...), custom_call_target="tpu_custom_call" | custom-call | tf_op jit(solution)/shard_map/local_next/pallas_call | solution.py:473
  106.0 21.8 %comm_last.1 = (f32[6,8,128]{2,1,0:T(8,128)S(1)}, f32[8,128]{1,0:T(8,128)S(1)}, f32[8,1280]{1,0:T(8,128)S(1)}) custom-call(f32[1,128]{1,0:T(1,128)S(1)} %bitcast.30, f32[32,64,128]{2,1,0:T(8,128)S(1)} %get-tuple-element.45.refs_1_, f32[2,32,128]{2,1,0:T(8,128)S(1)} %get-tuple-element.46.refs_2_, f32[8,5,8,128]{3,2,1,0:T(8,128)S(1)} %bitcast.25, ...), custom_call_target="tpu_custom_call" | custom-call | tf_op jit(solution)/shard_map/comm_last/pallas_call | solution.py:498
  127.8 1.2 multiply_add_fusion
  128.9 0.5 slice_bitcast_fusion
  129.5 0.6 copy.14
  (2 shorter events, 0.0 us)
Async XLA Ops:
  0.6 19.6 %copy-start.10 = (f32[128]{0:T(128)S(1)}, f32[128]{0:T(128)}, u32[]{:S(2)}) copy-start(f32[128]{0:T(128)} %param.16) | copy-start | bytes 1540
  0.6 43.1 %copy-start.5 = (s32[16384]{0:T(1024)S(1)}, s32[16384]{0:T(1024)}, u32[]{:S(2)}) copy-start(s32[16384]{0:T(1024)} %param.13) | copy-start | bytes 196612
  2.3 2.2 %copy-start = (bf16[16384,128]{1,0:T(8,128)(2,1)S(1)}, bf16[16384,128]{1,0:T(8,128)(2,1)}, u32[]{:S(2)}) copy-start(bf16[16384,128]{1,0:T(8,128)(2,1)} %jac_ref.5) | copy-start | bytes 12582916
  4.5 1.0 copy-start.2
  5.5 0.8 copy-start.4
  6.4 0.8 copy-start.6
  7.2 0.8 copy-start.7
  8.1 0.8 copy-start.8
  8.9 11.3 %copy-start.9 = (f32[8,1280]{1,0:T(8,128)S(1)}, f32[8,1280]{1,0:T(8,128)}, u32[]{:S(2)}) copy-start(f32[8,1280]{1,0:T(8,128)} %refs_4_.1) | copy-start | bytes 122884
  8.9 34.9 %copy-start.1 = (bf16[16384,128]{1,0:T(8,128)(2,1)S(1)}, bf16[16384,128]{1,0:T(8,128)(2,1)}, u32[]{:S(2)}) copy-start(bf16[16384,128]{1,0:T(8,128)(2,1)} %jac_ref.5) | copy-start | bytes 12582916
  8.9 34.9 %copy-start.3 = (f32[8,16384]{1,0:T(8,128)S(1)}, f32[8,16384]{1,0:T(8,128)}, u32[]{:S(2)}) copy-start(f32[8,16384]{1,0:T(8,128)} %pred_ref.5) | copy-start | bytes 1572868
